TPU v7x, 256 devices: a whole 4x4x8 slice. The times are simulated.
256 devices in a mesh: gx: 32 (over z_hi, x, core), gy: 8 (over y, z_lo).
Axes of the slice: x: 4, y: 4, z: 8 (z_hi: 4, z_lo: 2; z = z_hi * 2 + z_lo), core: 2. Of those that a mesh axis runs over, the one named last changes fastest.
Arguments:
- voltage: float32 [256, 256, 128], P('gx', 'gy'), may hold values from -0.5 to 1.5
- potential: float32 [256, 256, 128], P('gx', 'gy'), may hold values from -6 to 6
- tissue: int32 [256, 256, 128], P('gx', 'gy'), may hold values 0 or 1
- gain: float32 [256, 256, 128], P('gx', 'gy'), may hold values from 0.25 to 1.75
- couplings: float32 [2, 9], replicated, may hold values from 0.05 to 0.5
- line_factor: float32 [256, 256], replicated, as said below
Outputs:
- new_voltage: float32 [256, 256, 128], P('gx', 'gy')
- new_potential: float32 [256, 256, 128], P('gx', 'gy')
Inputs may be any that keep to these rules, and one draw needn't show every extreme that they name: line_factor is lower triangular with positive diagonal entries.
All inputs are finite; a program needn't handle non-finite values. No bound on the sum of `tissue` on one device may be relied on, other than what follows from the above.
Results may differ from a plain program's by a relative error of at most 0.0003.
Values sent between devices are 32-bit elements; how exact they have to be, the bound alone decides.
A program may use at most 64 MiB of HBM per device.

v0:
```python
import functools

import jax
import jax.numpy as jnp
from jax import lax
from jax.sharding import Mesh
from jax.sharding import PartitionSpec as P

CHEB = 8
ITERS = 4
GX_GY = ("gx_0", "gx_1", "gx_2", "gy_0", "gy_1")
GX = ("gx_0", "gx_1", "gx_2")
GY = ("gy_0", "gy_1")


highest = lax.Precision.HIGHEST
time_step = 2.0
ionic_rate = 0.5
onset_level = 0.2
gain_top = 3.0625
neighbours = (
    (1, 0, 0, 0),
    (-1, 0, 0, 0),
    (0, 1, 0, 1),
    (0, -1, 0, 1),
    (0, 0, 1, 2),
    (0, 0, -1, 2),
    (1, 1, 0, 3),
    (-1, -1, 0, 3),
    (1, -1, 0, 4),
    (-1, 1, 0, 4),
    (1, 0, 1, 5),
    (-1, 0, -1, 5),
    (1, 0, -1, 6),
    (-1, 0, 1, 6),
    (0, 1, 1, 7),
    (0, -1, -1, 7),
    (0, 1, -1, 8),
    (0, -1, 1, 8),
)
plane_order = (0, 1, 2)
line_order = (1, 2, 0)


def extended(cells, sides, width):
    for axis, dim in sides:
        count = lax.axis_size(axis)
        ends = count - 1
        head = lax.slice_in_dim(cells, 0, width, axis=dim)
        tail = lax.slice_in_dim(cells, cells.shape[dim] - width, cells.shape[dim], axis=dim)
        cells = jnp.concatenate(
            [
                lax.ppermute(tail, axis, [(i, (i + 1) % count) for i in range(ends)]),
                cells,
                lax.ppermute(head, axis, [((i + 1) % count, i) for i in range(ends)]),
            ],
            axis=dim,
        )
    return cells


def side_by_side(arrays, axis, split_dim, concat_dim, along):
    both = jnp.concatenate(arrays, axis=along)
    filled, at, gathered = (
        lax.all_to_all(both, axis, split_axis=split_dim, concat_axis=concat_dim, tiled=True),
        0,
        [],
    )
    for a in arrays:
        gathered.append(lax.slice_in_dim(filled, at, at + a.shape[along], axis=along))
        at += a.shape[along]
    return tuple(gathered)


def by_axis(array, axes):
    return functools.reduce(lax.psum, axes, array)


def shifted(padded, moves):
    extent = padded.shape
    return padded[
        1 + moves[0] : extent[0] - 1 + moves[0],
        1 + moves[1] : extent[1] - 1 + moves[1],
        1 + moves[2] : extent[2] - 1 + moves[2],
    ]


def fluxes(vector_pad, cond_pad, intra_coef, extra_coef, order):
    centre = shifted(vector_pad, (0, 0, 0))
    intra = jnp.zeros_like(centre)
    extra = jnp.zeros_like(centre)
    for move_z, move_y, move_x, column in neighbours:
        offset = (move_z, move_y, move_x)
        moves = (offset[order[0]], offset[order[1]], offset[order[2]])
        difference = centre - shifted(vector_pad, moves)
        intra = intra + intra_coef[column] * shifted(cond_pad, moves) * difference
        extra = extra + extra_coef[column] * difference
    return (shifted(cond_pad, (0, 0, 0)) * intra, extra)


def along_lines_minor(vector, line_factor):
    extent = vector.shape
    matrix = vector.reshape(-1, extent[2])
    first = jnp.dot(matrix, line_factor.T, precision=highest)
    second = jnp.dot(first, line_factor, precision=highest)
    return second.reshape(extent)


def pad_plane_x(array):
    return jnp.pad(array, ((0, 0), (0, 0), (1, 1)))


def pad_line_z(array):
    return jnp.pad(array, ((0, 0), (0, 0), (1, 1)))


def body(voltage, potential, tissue, gain, couplings, line_factor):
    mask_f = tissue.astype(jnp.float32)
    conduct = mask_f * gain
    intra_coef = couplings[0]
    extra_coef = couplings[1]
    cond_pad = pad_plane_x(extended(conduct, ((GX, 0), (GY, 1)), 1))
    volt_rim, pot_rim = (
        extended(voltage, ((GX, 0), (GY, 1)), 1),
        extended(potential, ((GX, 0), (GY, 1)), 1),
    )
    volt_intra, volt_extra = fluxes(
        pad_plane_x(volt_rim), cond_pad, intra_coef, extra_coef, plane_order
    )
    pot_intra, pot_extra = fluxes(
        pad_plane_x(pot_rim), cond_pad, intra_coef, extra_coef, plane_order
    )
    ionic = mask_f * voltage * (voltage - onset_level) * (voltage - 1.0)
    source = voltage - ionic_rate * ionic - time_step * pot_intra
    residual = source - (voltage + time_step * volt_intra)
    top_eig = 1.0 + time_step * 4.0 * gain_top * jnp.sum(intra_coef)
    centre_eig = (top_eig + 1.0) / 2.0
    half_width = (top_eig - 1.0) / 2.0
    spread_ratio = centre_eig / half_width
    weight_now = 1.0 / spread_ratio
    update = residual / centre_eig
    estimate = voltage
    for sweep in range(CHEB):
        estimate = estimate + update
        if sweep < CHEB - 1:
            upd_rim = extended(update, ((GX, 0), (GY, 1)), 1)
            upd_intra, upd_extra = fluxes(
                pad_plane_x(upd_rim), cond_pad, intra_coef, extra_coef, plane_order
            )
            residual = residual - (update + time_step * upd_intra)
            weight_next = 1.0 / (2.0 * spread_ratio - weight_now)
            update = weight_next * weight_now * update + 2.0 * weight_next / half_width * residual
            weight_now = weight_next
    est_rim = extended(estimate, ((GX, 0), (GY, 1)), 1)
    est_intra, est_extra = fluxes(
        pad_plane_x(est_rim), cond_pad, intra_coef, extra_coef, plane_order
    )
    residual = -est_intra - (pot_intra + pot_extra)
    residual, approx, cond_lines = side_by_side((residual, potential, conduct), GX, 2, 0, 1)
    residual = jnp.transpose(residual, (1, 2, 0))
    approx = jnp.transpose(approx, (1, 2, 0))
    cond_lines = jnp.transpose(cond_lines, (1, 2, 0))
    line_cond_pad = pad_line_z(extended(cond_lines, ((GX, 1), (GY, 0)), 1))

    def operate_elliptic(vector):
        vector_pad = pad_line_z(extended(vector, ((GX, 1), (GY, 0)), 1))
        image_intra, image_extra = fluxes(
            vector_pad, line_cond_pad, intra_coef, extra_coef, line_order
        )
        return image_intra + image_extra

    def precondition(vector):
        return along_lines_minor(vector, line_factor)

    def joint_products(first, second, third):
        return (by_axis(jnp.sum(first * second), GX_GY), by_axis(jnp.sum(third * second), GX_GY))

    smoothed = precondition(residual)
    image = operate_elliptic(smoothed)
    energy, curvature = joint_products(residual, smoothed, image)
    step_size = energy / curvature
    search = smoothed
    along = image
    for turn in range(ITERS):
        approx = approx + step_size * search
        if turn < ITERS - 1:
            residual = residual - step_size * along
            smoothed = precondition(residual)
            image = operate_elliptic(smoothed)
            energy_new, curvature = joint_products(residual, smoothed, image)
            step_ratio = energy_new / energy
            step_size = energy_new / (curvature - step_ratio * energy_new / step_size)
            search = smoothed + step_ratio * search
            along = image + step_ratio * along
            energy = energy_new
    approx = lax.all_to_all(
        jnp.transpose(approx, (2, 0, 1)), GX, split_axis=0, concat_axis=2, tiled=True
    )
    return (estimate, approx)


def solution(mesh):
    finer = Mesh(mesh.devices.reshape(4, 4, 2, 4, 2), ("gx_0", "gx_1", "gx_2", "gy_0", "gy_1"))
    in_specs = (P(GX, GY, None), P(GX, GY, None), P(GX, GY, None), P(GX, GY, None), P(), P())
    out_specs = (P(GX, GY, None), P(GX, GY, None))
    return jax.shard_map(body, mesh=finer, in_specs=in_specs, out_specs=out_specs, check_vma=False)
```

profile of v0, /device:TPU:1, one launch (start us, length us, event | category | flops | bytes accessed | tf_op | source)
XLA Modules:
  0.0 645.9 jit_solution(6930180787713141720)
XLA Ops:
  1.5 5.1 collective-permute-start.1
  12.6 3.3 collective-permute-start.2
  19.8 3.6 collective-permute-start.9
  27.8 4.0 collective-permute-start.11
  33.3 4.3 collective-permute-start.7
  39.1 3.7 collective-permute-done.5
  43.4 6.7 %fusion.554 = (f32[8,32,128]{2,1,0:T(8,128)S(1)}, f32[8,32,128]{2,1,0:T(8,128)S(1)}, f32[8,32,128]{2,1,0:T(8,128)S(1)}) fusion(f32[8,32,128]{2,1,0:T(8,128)S(1)} %copy-done.1, s32[8,32,128]{2,1,0:T(8,128)S(1)} %copy-done.3, f32[]{:T(128)S(6)} %div.90, f32[8,32,128]{2,1,0:T(8,128)S(1)} %convert_multiply_fusion, f32[8,32,128]{2,1,0:T(8,128)S(1)} %copy-done.4, ...), kind=kLoop, calls=%fused_computation.969 | loop fusion | flops 5177344 | bytes 6082600 | tf_op jit(solution)/shard_map/div | solution.py:141
  50.1 4.2 collective-permute-start.13
  59.4 4.5 collective-permute-start.15
  68.6 6.1 multiply_add_fusion.11
  74.7 3.4 collective-permute-start.17
  90.7 6.2 multiply_add_fusion.10
  96.9 6.8 %collective-permute-start.21 = (f32[1,32,128]{2,1,0:T(8,128)S(1)}, f32[1,32,128]{2,1,0:T(8,128)S(1)}, u32[]{:S(2)}, u32[]{:S(2)}) collective-permute-start(f32[1,32,128]{2,1,0:T(8,128)S(1)} %get-tuple-element.160), channel_id=1, source_target_pairs={{0,8},{8,16},{16,24},{24,32},{32,40},{40,48},{48,56},{56,64},{64,7... | collective-permute-start | bytes 49160 | tf_op jit(solution)/shard_map/ppermute | solution.py:53
  108.8 4.5 collective-permute-start.23
  118.0 6.1 multiply_add_fusion.9
  124.1 8.7 %collective-permute-start.25 = (f32[1,32,128]{2,1,0:T(8,128)S(1)}, f32[1,32,128]{2,1,0:T(8,128)S(1)}, u32[]{:S(2)}, u32[]{:S(2)}) collective-permute-start(f32[1,32,128]{2,1,0:T(8,128)S(1)} %get-tuple-element.158), channel_id=1, source_target_pairs={{0,8},{8,16},{16,24},{24,32},{32,40},{40,48},{48,56},{56,64},{64,7... | collective-permute-start | bytes 49160 | tf_op jit(solution)/shard_map/ppermute | solution.py:53
  134.7 4.1 collective-permute-done.24
  146.4 6.1 multiply_add_fusion.8
  152.5 5.1 collective-permute-start.29
  159.6 4.4 collective-permute-done.28
  164.0 4.3 collective-permute-start.31
  172.8 6.8 %multiply_add_fusion.7 = (f32[8,32,128]{2,1,0:T(8,128)S(1)}, f32[8,32,128]{2,1,0:T(8,128)}) fusion(f32[8,32,128]{2,1,0:T(8,128)S(1)} %get-tuple-element.70, f32[8,32,128]{2,1,0:T(8,128)S(1)} %get-tuple-element.71, f32[]{:T(128)S(6)} %div.105, f32[]{:T(128)S(6)} %mul.2259, f32[]{:T(128)S(6)} %div.103, f32[8,32,128]{2,1,0:T(8,128)S(1)} %get-tuple-element.69, ...), kind=kLoop, calls=%fused_computation.959 | loop fusion | flops 2752512 | bytes 5046320 | tf_op jit(solution)/shard_map/add | solution.py:152
  179.6 5.4 collective-permute-start.33
  187.0 4.1 collective-permute-done.32
  199.4 6.8 %multiply_add_fusion.6 = (f32[8,32,128]{2,1,0:T(8,128)S(1)}, f32[8,32,128]{2,1,0:T(8,128)}) fusion(f32[8,32,128]{2,1,0:T(8,128)S(1)} %copy-done.7, f32[8,32,128]{2,1,0:T(8,128)S(1)} %get-tuple-element.70, f32[8,32,128]{2,1,0:T(8,128)S(1)} %get-tuple-element.71, f32[]{:T(128)S(6)} %div.107, f32[]{:T(128)S(6)} %mul.2285, f32[]{:T(128)S(6)} %div.105, ...), kind=kLoop, calls=%fused_computation.958 | loop fusion | flops 2850816 | bytes 5177400 | tf_op jit(solution)/shard_map/add | solution.py:152
  206.2 5.1 collective-permute-start.37
  213.3 4.4 collective-permute-done.36
  226.1 6.3 fusion.137
  232.4 4.9 collective-permute-start.41
  239.4 4.5 collective-permute-done.40
  252.0 12.4 %fusion.93 = f32[8,32,128]{2,1,0:T(8,128)S(1)} fusion(f32[8,32,128]{2,1,0:T(8,128)S(1)} %convert_multiply_fusion, f32[8,32,128]{2,1,0:T(8,128)S(1)} %fusion.137, f32[10,34,130]{2,1,0:T(8,128)S(1)} %select_maximum_fusion, f32[10,33,128]{2,1,0:T(8,128)S(1)} %get-tuple-element.99, f32[10,33,128]{2,1,0:T(8,128)S(1)} %get-tuple-element.98, ...), kind=kLoop, calls=%fused_computation.295 | loop fusion | flops 5734400 | bytes 6301768 | tf_op jit(solution)/shard_map/sub | solution.py:158
  264.7 52.1 %all_to_all.36 = f32[8,96,128]{1,0,2:T(8,128)S(1)} all-to-all(f32[8,96,128]{1,0,2:T(8,128)S(1)} %copy.1161), channel_id=1, replica_groups=mesh['gx_0'=4,'gx_1'=4,'gx_2'=2,'gy_0'=4,'gy_1'=2] {'gx_0','gx_1','gx_2'}, dimensions={2} | all-to-all | bytes 786432 | tf_op jit(solution)/shard_map/all_to_all | solution.py:65
  325.6 3.6 collective-permute-start.48
  330.6 4.0 collective-permute-start.46
  336.0 4.5 collective-permute-start.50
  341.4 12.6 %multiply_reduce_fusion.5 = (f32[]{:T(128)}, f32[]{:T(128)}, f32[32,4,256]{2,0,1:T(8,128)S(1)}) fusion(f32[32,4,256]{2,1,0:T(4,128)S(1)} %reshape.65, f32[256,32,4]{0,1,2:T(8,128)S(1)} %copy.1280, f32[]{:T(128)} %bitcast.17, f32[]{:T(128)} %bitcast.16, f32[]{:T(128)} %bitcast.15, f32[]{:T(128)} %bitcast.14, f32[]{:T(128)} %bitcast.13, f32[]{:T(128)} %bitcast.12, ...), kind=kLoop, calls=%fused_computation.957 | loop fusion | flops 3964926 | bytes 4403280 | tf_op jit(solution)/shard_map/reduce_sum | solution.py:176
  354.0 11.5 %all-reduce.27 = (f32[]{:T(128)}, f32[]{:T(128)}) all-reduce(f32[]{:T(128)} %get-tuple-element.21, f32[]{:T(128)} %get-tuple-element.20), channel_id=1, replica_groups=mesh['gx_0'=4,'gx_1'=4,'gx_2'=2,'gy_0'=4,'gy_1'=2] {'gx_0'}, use_global_device_ids=true, to_apply=%region_2.3 | all-reduce | flops 2 | bytes 16 | tf_op jit(solution)/shard_map/psum | solution.py:76
  365.6 11.0 %all-reduce.23 = (f32[]{:T(128)}, f32[]{:T(128)}) all-reduce(f32[]{:T(128)} %get-tuple-element.44, f32[]{:T(128)} %get-tuple-element.45), channel_id=1, replica_groups=mesh['gx_0'=4,'gx_1'=4,'gx_2'=2,'gy_0'=4,'gy_1'=2] {'gx_1'}, use_global_device_ids=true, to_apply=%region_3.4 | all-reduce | flops 2 | bytes 16 | tf_op jit(solution)/shard_map/psum | solution.py:76
  376.6 4.1 all-reduce.35
  380.7 11.0 %all-reduce.19 = (f32[]{:T(128)}, f32[]{:T(128)}) all-reduce(f32[]{:T(128)} %get-tuple-element.60, f32[]{:T(128)} %get-tuple-element.61), channel_id=1, replica_groups=mesh['gx_0'=4,'gx_1'=4,'gx_2'=2,'gy_0'=4,'gy_1'=2] {'gy_0'}, use_global_device_ids=true, to_apply=%region_5.6 | all-reduce | flops 2 | bytes 16 | tf_op jit(solution)/shard_map/psum | solution.py:76
  391.7 4.5 all-reduce.31
  398.5 7.0 %collective-permute-start.52 = (f32[32,1,256]{2,0,1:T(8,128)S(1)}, f32[32,1,256]{2,0,1:T(8,128)S(1)}, u32[]{:S(2)}, u32[]{:S(2)}) collective-permute-start(f32[32,1,256]{2,0,1:T(8,128)S(1)} %get-tuple-element.145), channel_id=1, source_target_pairs={{0,8},{8,16},{16,24},{24,32},{32,40},{40,48},{48,56},{56,64},{64,7... | collective-permute-start | bytes 98312 | tf_op jit(solution)/shard_map/ppermute | solution.py:53
  412.1 4.0 collective-permute-start.54
  417.1 12.6 %multiply_reduce_fusion.3 = (f32[]{:T(128)}, f32[]{:T(128)}, f32[32,4,256]{2,0,1:T(8,128)S(1)}) fusion(f32[32,4,256]{2,1,0:T(4,128)S(1)} %reshape.67, f32[32,4,256]{2,0,1:T(8,128)S(1)} %bitcast_subtract_fusion, f32[]{:T(128)} %bitcast.17, f32[]{:T(128)} %bitcast.16, f32[]{:T(128)} %bitcast.15, f32[]{:T(128)} %bitcast.14, f32[]{:T(128)} %bitcast.13, ...), kind=kLoop, calls=%fused_computation.955 | loop fusion | flops 3964926 | bytes 4403280 | tf_op jit(solution)/shard_map/reduce_sum | solution.py:176
  429.7 9.6 %all-reduce.26 = (f32[]{:T(128)}, f32[]{:T(128)}) all-reduce(f32[]{:T(128)} %get-tuple-element.19, f32[]{:T(128)} %get-tuple-element.18), channel_id=1, replica_groups=mesh['gx_0'=4,'gx_1'=4,'gx_2'=2,'gy_0'=4,'gy_1'=2] {'gx_0'}, use_global_device_ids=true, to_apply=%region_14.15 | all-reduce | flops 2 | bytes 16 | tf_op jit(solution)/shard_map/psum | solution.py:76
  439.3 12.1 %all-reduce.22 = (f32[]{:T(128)}, f32[]{:T(128)}) all-reduce(f32[]{:T(128)} %get-tuple-element.42, f32[]{:T(128)} %get-tuple-element.43), channel_id=1, replica_groups=mesh['gx_0'=4,'gx_1'=4,'gx_2'=2,'gy_0'=4,'gy_1'=2] {'gx_1'}, use_global_device_ids=true, to_apply=%region_15.16 | all-reduce | flops 2 | bytes 16 | tf_op jit(solution)/shard_map/psum | solution.py:76
  451.4 3.6 all-reduce.34
  455.1 9.0 %all-reduce.18 = (f32[]{:T(128)}, f32[]{:T(128)}) all-reduce(f32[]{:T(128)} %get-tuple-element.58, f32[]{:T(128)} %get-tuple-element.59), channel_id=1, replica_groups=mesh['gx_0'=4,'gx_1'=4,'gx_2'=2,'gy_0'=4,'gy_1'=2] {'gy_0'}, use_global_device_ids=true, to_apply=%region_17.18 | all-reduce | flops 2 | bytes 16 | tf_op jit(solution)/shard_map/psum | solution.py:76
  464.1 4.4 all-reduce.30
  474.1 7.0 %collective-permute-start.56 = (f32[32,1,256]{2,0,1:T(8,128)S(1)}, f32[32,1,256]{2,0,1:T(8,128)S(1)}, u32[]{:S(2)}, u32[]{:S(2)}) collective-permute-start(f32[32,1,256]{2,0,1:T(8,128)S(1)} %get-tuple-element.143), channel_id=1, source_target_pairs={{0,8},{8,16},{16,24},{24,32},{32,40},{40,48},{48,56},{56,64},{64,7... | collective-permute-start | bytes 98312 | tf_op jit(solution)/shard_map/ppermute | solution.py:53
  487.7 4.0 collective-permute-start.58
  492.7 12.6 %multiply_reduce_fusion.1 = (f32[]{:T(128)}, f32[]{:T(128)}, f32[32,4,256]{2,0,1:T(8,128)S(1)}) fusion(f32[32,4,256]{2,1,0:T(4,128)S(1)} %reshape.69, f32[32,4,256]{2,0,1:T(8,128)S(1)} %multiply_subtract_fusion.1, f32[]{:T(128)} %bitcast.17, f32[]{:T(128)} %bitcast.16, f32[]{:T(128)} %bitcast.15, f32[]{:T(128)} %bitcast.14, f32[]{:T(128)} %bitcast.13, ...), kind=kLoop, calls=%fused_computation.951 | loop fusion | flops 3964926 | bytes 4403280 | tf_op jit(solution)/shard_map/reduce_sum | solution.py:176
  505.3 9.3 %all-reduce.25 = (f32[]{:T(128)}, f32[]{:T(128)}) all-reduce(f32[]{:T(128)} %get-tuple-element.17, f32[]{:T(128)} %get-tuple-element.16), channel_id=1, replica_groups=mesh['gx_0'=4,'gx_1'=4,'gx_2'=2,'gy_0'=4,'gy_1'=2] {'gx_0'}, use_global_device_ids=true, to_apply=%region_26.27 | all-reduce | flops 2 | bytes 16 | tf_op jit(solution)/shard_map/psum | solution.py:76
  514.6 12.5 %all-reduce.21 = (f32[]{:T(128)}, f32[]{:T(128)}) all-reduce(f32[]{:T(128)} %get-tuple-element.40, f32[]{:T(128)} %get-tuple-element.41), channel_id=1, replica_groups=mesh['gx_0'=4,'gx_1'=4,'gx_2'=2,'gy_0'=4,'gy_1'=2] {'gx_1'}, use_global_device_ids=true, to_apply=%region_27.28 | all-reduce | flops 2 | bytes 16 | tf_op jit(solution)/shard_map/psum | solution.py:76
  530.3 8.9 %all-reduce.17 = (f32[]{:T(128)}, f32[]{:T(128)}) all-reduce(f32[]{:T(128)} %get-tuple-element.56, f32[]{:T(128)} %get-tuple-element.57), channel_id=1, replica_groups=mesh['gx_0'=4,'gx_1'=4,'gx_2'=2,'gy_0'=4,'gy_1'=2] {'gy_0'}, use_global_device_ids=true, to_apply=%region_29.30 | all-reduce | flops 2 | bytes 16 | tf_op jit(solution)/shard_map/psum | solution.py:76
  539.3 4.7 all-reduce.29
  549.0 7.0 %collective-permute-start.60 = (f32[32,1,256]{2,0,1:T(8,128)S(1)}, f32[32,1,256]{2,0,1:T(8,128)S(1)}, u32[]{:S(2)}, u32[]{:S(2)}) collective-permute-start(f32[32,1,256]{2,0,1:T(8,128)S(1)} %get-tuple-element.139), channel_id=1, source_target_pairs={{0,8},{8,16},{16,24},{24,32},{32,40},{40,48},{48,56},{56,64},{64,7... | collective-permute-start | bytes 98312 | tf_op jit(solution)/shard_map/ppermute | solution.py:53
  562.6 4.0 collective-permute-start.62
  567.5 12.6 %fusion.557 = f32[]{:T(128)} fusion(f32[32,4,256]{2,0,1:T(8,128)S(1)} %copy.1249, f32[32,4,256]{2,0,1:T(8,128)S(1)} %bitcast.75, f32[32,6,256]{2,0,1:T(8,128)S(1)} %constant_dynamic-update-slice_fusion.15, f32[1,6,256]{2,0,1:T(1,128)S(1)} %collective-permute-done.62, f32[1,6,256]{2,0,1:T(1,128)S(1)} %collective-permute-done.63, ...), kind=kLoop, calls=%fused_computation.974 | loop fusion | flops 3899391 | bytes 4010060 | tf_op jit(solution)/shard_map/reduce_sum | solution.py:176
  580.2 9.6 %all-reduce.24 = (f32[]{:T(128)}, f32[]{:T(128)}) all-reduce(f32[]{:T(128)} %get-tuple-element.141, f32[]{:T(128)} %fusion.557), channel_id=1, replica_groups=mesh['gx_0'=4,'gx_1'=4,'gx_2'=2,'gy_0'=4,'gy_1'=2] {'gx_0'}, use_global_device_ids=true, to_apply=%region_38.39 | all-reduce | flops 2 | bytes 16 | tf_op jit(solution)/shard_map/psum | solution.py:76
  589.7 12.5 %all-reduce.20 = (f32[]{:T(128)}, f32[]{:T(128)}) all-reduce(f32[]{:T(128)} %get-tuple-element.38, f32[]{:T(128)} %get-tuple-element.39), channel_id=1, replica_groups=mesh['gx_0'=4,'gx_1'=4,'gx_2'=2,'gy_0'=4,'gy_1'=2] {'gx_1'}, use_global_device_ids=true, to_apply=%region_39.40 | all-reduce | flops 2 | bytes 16 | tf_op jit(solution)/shard_map/psum | solution.py:76
  605.5 9.0 %all-reduce.16 = (f32[]{:T(128)}, f32[]{:T(128)}) all-reduce(f32[]{:T(128)} %get-tuple-element.54, f32[]{:T(128)} %get-tuple-element.55), channel_id=1, replica_groups=mesh['gx_0'=4,'gx_1'=4,'gx_2'=2,'gy_0'=4,'gy_1'=2] {'gy_0'}, use_global_device_ids=true, to_apply=%region_41.42 | all-reduce | flops 2 | bytes 16 | tf_op jit(solution)/shard_map/psum | solution.py:76
  614.4 4.5 all-reduce.28
  623.6 19.6 %all_to_all.37 = f32[32,1,1024]{2,1,0:T(1,128)S(1)} all-to-all(f32[32,1,1024]{2,1,0:T(1,128)S(1)} %reshape.72), channel_id=1, replica_groups=mesh['gx_0'=4,'gx_1'=4,'gx_2'=2,'gy_0'=4,'gy_1'=2] {'gx_0','gx_1','gx_2'}, dimensions={0} | all-to-all | bytes 262144 | tf_op jit(solution)/shard_map/all_to_all | solution.py:196
  (259 shorter events, 142.5 us)
Async XLA Ops:
  1.5 31.7 %collective-permute-start.1 = (f32[1,32,128]{2,1,0:T(8,128)S(1)}, f32[1,32,128]{2,1,0:T(8,128)S(1)}, u32[]{:S(2)}, u32[]{:S(2)}) collective-permute-start(f32[1,32,128]{2,1,0:T(8,128)S(1)} %get-tuple-element.170), channel_id=1, source_target_pairs={{8,0},{16,8},{24,16},{32,24},{40,32},{48,40},{56,48},{64,56},{72,6... | collective-permute-start | bytes 49160 | tf_op jit(solution)/shard_map/ppermute | solution.py:55
  6.6 25.3 %collective-permute-start.3 = (f32[1,32,128]{2,1,0:T(8,128)S(1)}, f32[1,32,128]{2,1,0:T(8,128)S(1)}, u32[]{:S(2)}, u32[]{:S(2)}) collective-permute-start(f32[1,32,128]{2,1,0:T(8,128)S(1)} %get-tuple-element.171), channel_id=1, source_target_pairs={{0,8},{8,16},{16,24},{24,32},{32,40},{40,48},{48,56},{56,64},{64,7... | collective-permute-start | bytes 49160 | tf_op jit(solution)/shard_map/ppermute | solution.py:53
  9.2 18.6 %collective-permute-start.8 = (f32[1,32,128]{2,1,0:T(8,128)S(1)}, f32[1,32,128]{2,1,0:T(8,128)S(1)}, u32[]{:S(2)}, u32[]{:S(2)}) collective-permute-start(f32[1,32,128]{2,1,0:T(8,128)S(1)} %get-tuple-element.166), channel_id=1, source_target_pairs={{8,0},{16,8},{24,16},{32,24},{40,32},{48,40},{56,48},{64,56},{72,6... | collective-permute-start | bytes 49160 | tf_op jit(solution)/shard_map/ppermute | solution.py:55
  12.6 7.2 %collective-permute-start.2 = (f32[1,32,128]{2,1,0:T(8,128)S(1)}, f32[1,32,128]{2,1,0:T(8,128)S(1)}, u32[]{:S(2)}, u32[]{:S(2)}) collective-permute-start(f32[1,32,128]{2,1,0:T(8,128)S(1)} %get-tuple-element.168), channel_id=1, source_target_pairs={{0,8},{8,16},{16,24},{24,32},{32,40},{40,48},{48,56},{56,64},{64,7... | collective-permute-start | bytes 49160 | tf_op jit(solution)/shard_map/ppermute | solution.py:53
  15.9 7.6 %collective-permute-start = (f32[1,32,128]{2,1,0:T(8,128)S(1)}, f32[1,32,128]{2,1,0:T(8,128)S(1)}, u32[]{:S(2)}, u32[]{:S(2)}) collective-permute-start(f32[1,32,128]{2,1,0:T(8,128)S(1)} %get-tuple-element.169), channel_id=1, source_target_pairs={{8,0},{16,8},{24,16},{32,24},{40,32},{48,40},{56,48},{64,56},{72,6... | collective-permute-start | bytes 49160 | tf_op jit(solution)/shard_map/ppermute | solution.py:55
  19.8 6.6 %collective-permute-start.9 = (f32[1,32,128]{2,1,0:T(8,128)S(1)}, f32[1,32,128]{2,1,0:T(8,128)S(1)}, u32[]{:S(2)}, u32[]{:S(2)}) collective-permute-start(f32[1,32,128]{2,1,0:T(8,128)S(1)} %get-tuple-element.167), channel_id=1, source_target_pairs={{0,8},{8,16},{16,24},{24,32},{32,40},{40,48},{48,56},{56,64},{64,7... | collective-permute-start | bytes 49160 | tf_op jit(solution)/shard_map/ppermute | solution.py:53
  23.5 14.0 %collective-permute-start.6 = (f32[10,1,128]{2,1,0:T(1,128)S(1)}, f32[10,1,128]{2,1,0:T(1,128)S(1)}, u32[]{:S(2)}, u32[]{:S(2)}) collective-permute-start(f32[10,1,128]{2,1,0:T(1,128)S(1)} %get-tuple-element.134), channel_id=1, source_target_pairs={{0,1},{1,2},{2,3},{3,4},{4,5},{5,6},{6,7},{8,9},{9,10},{10,11},{11... | collective-permute-start | bytes 15368 | tf_op jit(solution)/shard_map/ppermute | solution.py:53
  26.5 12.4 %collective-permute-start.4 = (f32[10,1,128]{2,1,0:T(1,128)S(1)}, f32[10,1,128]{2,1,0:T(1,128)S(1)}, u32[]{:S(2)}, u32[]{:S(2)}) collective-permute-start(f32[10,1,128]{2,1,0:T(1,128)S(1)} %get-tuple-element.135), channel_id=1, source_target_pairs={{1,0},{2,1},{3,2},{4,3},{5,4},{6,5},{7,6},{9,8},{10,9},{11,10},{12... | collective-permute-start | bytes 15368 | tf_op jit(solution)/shard_map/ppermute | solution.py:55
  27.8 15.2 %collective-permute-start.11 = (f32[10,1,128]{2,1,0:T(1,128)S(1)}, f32[10,1,128]{2,1,0:T(1,128)S(1)}, u32[]{:S(2)}, u32[]{:S(2)}) collective-permute-start(f32[10,1,128]{2,1,0:T(1,128)S(1)} %get-tuple-element.130), channel_id=1, source_target_pairs={{0,1},{1,2},{2,3},{3,4},{4,5},{5,6},{6,7},{8,9},{9,10},{10,11},{11... | collective-permute-start | bytes 15368 | tf_op jit(solution)/shard_map/ppermute | solution.py:53
  31.9 11.2 %collective-permute-start.10 = (f32[10,1,128]{2,1,0:T(1,128)S(1)}, f32[10,1,128]{2,1,0:T(1,128)S(1)}, u32[]{:S(2)}, u32[]{:S(2)}) collective-permute-start(f32[10,1,128]{2,1,0:T(1,128)S(1)} %get-tuple-element.131), channel_id=1, source_target_pairs={{1,0},{2,1},{3,2},{4,3},{5,4},{6,5},{7,6},{9,8},{10,9},{11,10},{12... | collective-permute-start | bytes 15368 | tf_op jit(solution)/shard_map/ppermute | solution.py:55
  33.3 5.9 collective-permute-start.7
  37.6 5.3 collective-permute-start.5
  50.1 6.2 collective-permute-start.13
  54.3 5.1 collective-permute-start.12
  59.4 6.7 %collective-permute-start.15 = (f32[10,1,128]{2,1,0:T(1,128)S(1)}, f32[10,1,128]{2,1,0:T(1,128)S(1)}, u32[]{:S(2)}, u32[]{:S(2)}) collective-permute-start(f32[10,1,128]{2,1,0:T(1,128)S(1)} %get-tuple-element.128), channel_id=1, source_target_pairs={{0,1},{1,2},{2,3},{3,4},{4,5},{5,6},{6,7},{8,9},{9,10},{10,11},{11... | collective-permute-start | bytes 15368 | tf_op jit(solution)/shard_map/ppermute | solution.py:53
  63.9 4.4 collective-permute-start.14
  74.7 5.3 collective-permute-start.17
  78.1 5.1 collective-permute-start.16
  83.2 4.0 collective-permute-start.19
  85.8 4.6 collective-permute-start.18
  96.9 8.7 %collective-permute-start.21 = (f32[1,32,128]{2,1,0:T(8,128)S(1)}, f32[1,32,128]{2,1,0:T(8,128)S(1)}, u32[]{:S(2)}, u32[]{:S(2)}) collective-permute-start(f32[1,32,128]{2,1,0:T(8,128)S(1)} %get-tuple-element.160), channel_id=1, source_target_pairs={{0,8},{8,16},{16,24},{24,32},{32,40},{40,48},{48,56},{56,64},{64,7... | collective-permute-start | bytes 49160 | tf_op jit(solution)/shard_map/ppermute | solution.py:53
  103.7 5.1 collective-permute-start.20
  108.8 5.9 collective-permute-start.23
  113.3 4.4 collective-permute-start.22
  124.1 10.6 %collective-permute-start.25 = (f32[1,32,128]{2,1,0:T(8,128)S(1)}, f32[1,32,128]{2,1,0:T(8,128)S(1)}, u32[]{:S(2)}, u32[]{:S(2)}) collective-permute-start(f32[1,32,128]{2,1,0:T(8,128)S(1)} %get-tuple-element.158), channel_id=1, source_target_pairs={{0,8},{8,16},{16,24},{24,32},{32,40},{40,48},{48,56},{56,64},{64,7... | collective-permute-start | bytes 49160 | tf_op jit(solution)/shard_map/ppermute | solution.py:53
  132.8 6.0 collective-permute-start.24
  138.8 4.3 collective-permute-start.27
  141.7 4.4 collective-permute-start.26
  152.5 7.1 %collective-permute-start.29 = (f32[1,32,128]{2,1,0:T(8,128)S(1)}, f32[1,32,128]{2,1,0:T(8,128)S(1)}, u32[]{:S(2)}, u32[]{:S(2)}) collective-permute-start(f32[1,32,128]{2,1,0:T(8,128)S(1)} %get-tuple-element.156), channel_id=1, source_target_pairs={{0,8},{8,16},{16,24},{24,32},{32,40},{40,48},{48,56},{56,64},{64,7... | collective-permute-start | bytes 49160 | tf_op jit(solution)/shard_map/ppermute | solution.py:53
  157.6 6.3 collective-permute-start.28
  164.0 5.7 collective-permute-start.31
  168.2 4.4 collective-permute-start.30
  179.6 7.3 %collective-permute-start.33 = (f32[1,32,128]{2,1,0:T(8,128)S(1)}, f32[1,32,128]{2,1,0:T(8,128)S(1)}, u32[]{:S(2)}, u32[]{:S(2)}) collective-permute-start(f32[1,32,128]{2,1,0:T(8,128)S(1)} %get-tuple-element.154), channel_id=1, source_target_pairs={{0,8},{8,16},{16,24},{24,32},{32,40},{40,48},{48,56},{56,64},{64,7... | collective-permute-start | bytes 49160 | tf_op jit(solution)/shard_map/ppermute | solution.py:53
  185.1 6.0 collective-permute-start.32
  191.1 4.2 collective-permute-start.35
  193.9 4.4 collective-permute-start.34
  206.2 7.1 %collective-permute-start.37 = (f32[1,32,128]{2,1,0:T(8,128)S(1)}, f32[1,32,128]{2,1,0:T(8,128)S(1)}, u32[]{:S(2)}, u32[]{:S(2)}) collective-permute-start(f32[1,32,128]{2,1,0:T(8,128)S(1)} %get-tuple-element.152), channel_id=1, source_target_pairs={{0,8},{8,16},{16,24},{24,32},{32,40},{40,48},{48,56},{56,64},{64,7... | collective-permute-start | bytes 49160 | tf_op jit(solution)/shard_map/ppermute | solution.py:53
  211.3 6.3 collective-permute-start.36
  217.6 4.2 collective-permute-start.39
  220.5 4.4 collective-permute-start.38
  232.4 7.0 %collective-permute-start.41 = (f32[1,32,128]{2,1,0:T(8,128)S(1)}, f32[1,32,128]{2,1,0:T(8,128)S(1)}, u32[]{:S(2)}, u32[]{:S(2)}) collective-permute-start(f32[1,32,128]{2,1,0:T(8,128)S(1)} %get-tuple-element.150), channel_id=1, source_target_pairs={{0,8},{8,16},{16,24},{24,32},{32,40},{40,48},{48,56},{56,64},{64,7... | collective-permute-start | bytes 49160 | tf_op jit(solution)/shard_map/ppermute | solution.py:53
  237.2 6.6 %collective-permute-start.40 = (f32[1,32,128]{2,1,0:T(8,128)S(1)}, f32[1,32,128]{2,1,0:T(8,128)S(1)}, u32[]{:S(2)}, u32[]{:S(2)}) collective-permute-start(f32[1,32,128]{2,1,0:T(8,128)S(1)} %get-tuple-element.151), channel_id=1, source_target_pairs={{8,0},{16,8},{24,16},{32,24},{40,32},{48,40},{56,48},{64,56},{72,6... | collective-permute-start | bytes 49160 | tf_op jit(solution)/shard_map/ppermute | solution.py:55
  243.8 4.1 collective-permute-start.43
  246.7 4.4 collective-permute-start.42
  317.4 11.8 %collective-permute-start.44 = (f32[32,1,256]{2,0,1:T(8,128)S(1)}, f32[32,1,256]{2,0,1:T(8,128)S(1)}, u32[]{:S(2)}, u32[]{:S(2)}) collective-permute-start(f32[32,1,256]{2,0,1:T(8,128)S(1)} %get-tuple-element.146), channel_id=1, source_target_pairs={{0,8},{8,16},{16,24},{24,32},{32,40},{40,48},{48,56},{56,64},{64,7... | collective-permute-start | bytes 98312 | tf_op jit(solution)/shard_map/ppermute | solution.py:53
  320.5 8.7 %collective-permute-start.45 = (f32[32,1,256]{2,0,1:T(8,128)S(1)}, f32[32,1,256]{2,0,1:T(8,128)S(1)}, u32[]{:S(2)}, u32[]{:S(2)}) collective-permute-start(f32[32,1,256]{2,0,1:T(8,128)S(1)} %get-tuple-element.147), channel_id=1, source_target_pairs={{8,0},{16,8},{24,16},{32,24},{40,32},{48,40},{56,48},{64,56},{72,6... | collective-permute-start | bytes 98312 | tf_op jit(solution)/shard_map/ppermute | solution.py:55
  323.6 11.0 %collective-permute-start.49 = (f32[32,1,256]{2,0,1:T(8,128)S(1)}, f32[32,1,256]{2,0,1:T(8,128)S(1)}, u32[]{:S(2)}, u32[]{:S(2)}) collective-permute-start(f32[32,1,256]{2,0,1:T(8,128)S(1)} %get-tuple-element.148), channel_id=1, source_target_pairs={{8,0},{16,8},{24,16},{32,24},{40,32},{48,40},{56,48},{64,56},{72,6... | collective-permute-start | bytes 98312 | tf_op jit(solution)/shard_map/ppermute | solution.py:55
  325.6 9.0 %collective-permute-start.48 = (f32[32,1,256]{2,0,1:T(8,128)S(1)}, f32[32,1,256]{2,0,1:T(8,128)S(1)}, u32[]{:S(2)}, u32[]{:S(2)}) collective-permute-start(f32[32,1,256]{2,0,1:T(8,128)S(1)} %get-tuple-element.149), channel_id=1, source_target_pairs={{0,8},{8,16},{16,24},{24,32},{32,40},{40,48},{48,56},{56,64},{64,7... | collective-permute-start | bytes 98312 | tf_op jit(solution)/shard_map/ppermute | solution.py:53
  329.3 11.2 %collective-permute-start.47 = (f32[1,6,256]{2,0,1:T(1,128)S(1)}, f32[1,6,256]{2,0,1:T(1,128)S(1)}, u32[]{:S(2)}, u32[]{:S(2)}) collective-permute-start(f32[1,6,256]{2,0,1:T(1,128)S(1)} %get-tuple-element.94), channel_id=1, source_target_pairs={{1,0},{2,1},{3,2},{4,3},{5,4},{6,5},{7,6},{9,8},{10,9},{11,10},{12... | collective-permute-start | bytes 18440 | tf_op jit(solution)/shard_map/ppermute | solution.py:55
  330.6 9.9 %collective-permute-start.46 = (f32[1,6,256]{2,0,1:T(1,128)S(1)}, f32[1,6,256]{2,0,1:T(1,128)S(1)}, u32[]{:S(2)}, u32[]{:S(2)}) collective-permute-start(f32[1,6,256]{2,0,1:T(1,128)S(1)} %get-tuple-element.95), channel_id=1, source_target_pairs={{0,1},{1,2},{2,3},{3,4},{4,5},{5,6},{6,7},{8,9},{9,10},{10,11},{11... | collective-permute-start | bytes 18440 | tf_op jit(solution)/shard_map/ppermute | solution.py:53
  334.7 6.0 collective-permute-start.51
  336.0 5.2 collective-permute-start.50
  398.5 9.0 %collective-permute-start.52 = (f32[32,1,256]{2,0,1:T(8,128)S(1)}, f32[32,1,256]{2,0,1:T(8,128)S(1)}, u32[]{:S(2)}, u32[]{:S(2)}) collective-permute-start(f32[32,1,256]{2,0,1:T(8,128)S(1)} %get-tuple-element.145), channel_id=1, source_target_pairs={{0,8},{8,16},{16,24},{24,32},{32,40},{40,48},{48,56},{56,64},{64,7... | collective-permute-start | bytes 98312 | tf_op jit(solution)/shard_map/ppermute | solution.py:53
  405.6 5.2 collective-permute-start.53
  410.8 5.3 collective-permute-start.55
  412.1 4.8 collective-permute-start.54
  474.1 9.0 %collective-permute-start.56 = (f32[32,1,256]{2,0,1:T(8,128)S(1)}, f32[32,1,256]{2,0,1:T(8,128)S(1)}, u32[]{:S(2)}, u32[]{:S(2)}) collective-permute-start(f32[32,1,256]{2,0,1:T(8,128)S(1)} %get-tuple-element.143), channel_id=1, source_target_pairs={{0,8},{8,16},{16,24},{24,32},{32,40},{40,48},{48,56},{56,64},{64,7... | collective-permute-start | bytes 98312 | tf_op jit(solution)/shard_map/ppermute | solution.py:53
  481.1 5.2 collective-permute-start.57
  486.4 5.3 collective-permute-start.59
  487.7 4.8 collective-permute-start.58
  549.0 9.0 %collective-permute-start.60 = (f32[32,1,256]{2,0,1:T(8,128)S(1)}, f32[32,1,256]{2,0,1:T(8,128)S(1)}, u32[]{:S(2)}, u32[]{:S(2)}) collective-permute-start(f32[32,1,256]{2,0,1:T(8,128)S(1)} %get-tuple-element.139), channel_id=1, source_target_pairs={{0,8},{8,16},{16,24},{24,32},{32,40},{40,48},{48,56},{56,64},{64,7... | collective-permute-start | bytes 98312 | tf_op jit(solution)/shard_map/ppermute | solution.py:53
  556.0 5.2 collective-permute-start.61
  561.3 5.5 collective-permute-start.63
  562.6 4.8 collective-permute-start.62
  (19 other events, 433.1 us)
where the time goes:
time: 650 us; the launch traced here: 646 us
  blocking collectives  230 us (35%)
  starting transfers between devices  195 us (30%)
  other arithmetic  121 us (19%)
  waiting for transfers between devices  69.5 us (11%)
  between operations  18.5 us (3%)
  local copies, waits for them, and re-layouts  9.56 us (1%)
    psum x20, blocking collectives, by_axis(): return functools.reduce(lax.psum, axes, array)  158 us
    ppermute x32, starting transfers between devices, extended(): lax.ppermute(tail, axis, [(i, (i + 1) % count) for i in range(ends)])  139 us
    ppermute x32, waiting for transfers between devices, extended(): lax.ppermute(head, axis, [((i + 1) % count, i) for i in range(ends)])  66.9 us
    ppermute x32, starting transfers between devices, extended(): lax.ppermute(head, axis, [((i + 1) % count, i) for i in range(ends)])  55.2 us
    all_to_all x1, blocking collectives, side_by_side(): lax.all_to_all(both, axis, split_axis=split_dim, concat_axis=concat_dim,...  52.1 us
    reduce_sum x4, other arithmetic, joint_products(): jnp.sum(third * second)  50.5 us
    add x6, other arithmetic, body(): weight_next * weight_now * update  38.1 us
    all_to_all x1, blocking collectives, body(): lax.all_to_all(jnp.transpose(approx, (2, 0, 1)), GX, split_axis=0, concat...  19.6 us
  transfers between devices with their start and end apart: 64, of which 24 were waited for; matrix products, arithmetic and copies ran while one was open for 1% of the time, Pallas kernels for 0%

commit v1 on v0

v1 whole, which is shorter than its diff:
```python
import jax
import jax.numpy as jnp
from jax import lax
from jax.experimental import pallas as pl
from jax.experimental.pallas import tpu as pltpu
from jax.sharding import PartitionSpec as P

CHEB = 8
SHIFT = 1.3
BASIS = 4
MESH = pl.DeviceIdType.MESH
HIGHEST = lax.Precision.HIGHEST
time_step = 2.0
ionic_rate = 0.5
onset_level = 0.2
gain_top = 3.0625

PLANES, ROWS, COLS = 8, 32, 128
HALO = 8
EXT_Z, EXT_Y = PLANES + 2 * HALO, ROWS + 2 * HALO
GX, GY = 32, 8
WHOLE_Z = GX * PLANES
WHOLE_Y = GY * ROWS
TILES = WHOLE_Z // 8
DIRECTIONS = tuple((a, b) for a in (-1, 0, 1) for b in (-1, 0, 1) if (a, b) != (0, 0))


def z_range(a, depth):
    if a == 0:
        return pl.ds(HALO, PLANES), pl.ds(HALO, PLANES)
    if a > 0:
        return pl.ds(HALO + PLANES - depth, depth), pl.ds(HALO - depth, depth)
    return pl.ds(HALO, depth), pl.ds(HALO + PLANES, depth)


def y_range(b):
    if b == 0:
        return pl.ds(HALO, ROWS), pl.ds(HALO, ROWS)
    if b > 0:
        return pl.ds(HALO + ROWS - 8, 8), pl.ds(0, 8)
    return pl.ds(HALO, 8), pl.ds(HALO + ROWS, 8)


def lane_shifts(v, first, last):
    up = jnp.where(last, 0.0, pltpu.roll(v, COLS - 1, 1))
    down = jnp.where(first, 0.0, pltpu.roll(v, 1, 1))
    return up, down


def stencil(minus, here, plus, k, first, last, swapped=False):
    rows = here.shape[0]
    lead, sub, lane = (k[1], k[0], k[2]) if swapped else (k[0], k[1], k[2])
    both, cross = k[3], k[4]
    lead_lane, lead_lane_cross = (k[7], k[8]) if swapped else (k[5], k[6])
    sub_lane, sub_lane_cross = (k[5], k[6]) if swapped else (k[7], k[8])
    right, left = lane_shifts(here, first, last)
    up = sub * here + both * plus + cross * minus + sub_lane * right + sub_lane_cross * left
    down = sub * here + both * minus + cross * plus + sub_lane * left + sub_lane_cross * right
    x_up = lane * here + lead_lane * plus + lead_lane_cross * minus
    x_down = lane * here + lead_lane * minus + lead_lane_cross * plus
    x_up = jnp.where(last, 0.0, pltpu.roll(x_up, COLS - 1, 1))
    x_down = jnp.where(first, 0.0, pltpu.roll(x_down, 1, 1))
    return lead * (plus + minus) + pltpu.roll(up, rows - 1, 0) + pltpu.roll(down, 1, 0) + x_up + x_down


def owner(row):
    chip_y = row // 64
    along = row % 64
    along = along + (chip_y % 2) * (63 - 2 * along)
    chip_z = along // 8
    spot = along % 8
    spot = spot + (chip_z % 2) * (7 - 2 * spot)
    return (chip_z // 2) * 8 + spot, chip_y * 2 + chip_z % 2


def own_row(gx, gy):
    chip_y = gy // 2
    chip_z = (gx // 8) * 2 + gy % 2
    spot = gx % 8
    spot = spot + (chip_z % 2) * (7 - 2 * spot)
    along = chip_z * 8 + spot
    return chip_y * 64 + along + (chip_y % 2) * (63 - 2 * along)


def kernel(
    coup, volt_in, pot_in, tissue_in, gain_in, factor_in, new_volt, new_pot,
    volt, pot, tissue, gain, factor,
    fields, resid, upd, diag, ionic_own, matrix,
    stage_cond, stage_res, stage_row,
    row_cond, row_res, lines, line_prev, line_next, cond_prev, cond_next,
    image, row_diag, back, part, gather_a, gather_b,
    s_fields, r_fields, s_cond, r_cond, s_resid, r_resid,
    s_rows, r_rows, s_edge, r_edge, s_back, r_back, s_sum, r_sum, s_local, s_take,
):
    gx = lax.axis_index("gx")
    gy = lax.axis_index("gy")
    row = own_row(gx, gy)
    own_gy = row // ROWS
    own_t = row % ROWS
    me_a = ((gx % 8) // 2) * 4 + gy // 2
    me_b = (gx // 8) * 4 + (gy % 2) * 2 + gx % 2

    def peer_a(p):
        return (gx // 8) * 8 + (p // 4) * 2 + gx % 2, (p % 4) * 2 + gy % 2

    def peer_b(p):
        return (p // 4) * 8 + ((gx % 8) // 2) * 2 + p % 2, (gy // 2) * 2 + (p % 4) // 2

    barrier = pltpu.get_barrier_semaphore()

    def greet(to):
        pl.semaphore_signal(barrier, inc=1, device_id=to, device_id_type=MESH)

    for a, b in DIRECTIONS:
        greet((lax.rem(gx + a + GX, GX), lax.rem(gy + b + GY, GY)))
    greet(owner(lax.rem(row + 1, WHOLE_Y)))
    greet(owner(lax.rem(row + WHOLE_Y - 1, WHOLE_Y)))

    def greet_sixteen(d, _):
        greet(peer_a(lax.rem(me_a + d, 16)))
        greet(peer_b(lax.rem(me_b + d, 16)))
        return 0

    lax.fori_loop(1, 16, greet_sixteen, 0)

    def greet_rows(t, _):
        to_gx, to_gy = owner(gy * ROWS + t)

        @pl.when(jnp.logical_not((to_gx == gx) & (to_gy == gy)))
        def _():
            greet((to_gx, to_gy))

        @pl.when(jnp.logical_not((t == gx) & (own_gy == gy)))
        def _():
            greet((t, own_gy))
        return 0

    lax.fori_loop(0, ROWS, greet_rows, 0)
    takes = [
        pltpu.make_async_copy(src, dst, s_take.at[n])
        for n, (src, dst) in enumerate(
            ((tissue_in, tissue), (gain_in, gain), (volt_in, volt), (pot_in, pot), (factor_in, factor)))
    ]
    for copy in takes:
        copy.start()
    for copy in takes:
        copy.wait()

    lane = lax.broadcasted_iota(jnp.int32, (1, COLS), 1)
    first, last = lane == 0, lane == COLS - 1
    k_in = [coup[0, n] for n in range(9)]
    k_ex = [coup[1, n] for n in range(9)]

    def neighbour(a, b):
        ok = (gx + a >= 0) & (gx + a < GX) & (gy + b >= 0) & (gy + b < GY)
        return ok, (gx + a, gy + b)

    def send_halo(ref, d, depth, sems_s, sems_r, stacked):
        a, b = DIRECTIONS[d]
        zs, zd = z_range(a, depth)
        ys, yd = y_range(b)
        src = ref.at[:, zs, ys, :] if stacked else ref.at[zs, ys, :]
        dst = ref.at[:, zd, yd, :] if stacked else ref.at[zd, yd, :]
        return pltpu.make_async_remote_copy(
            src_ref=src, dst_ref=dst, send_sem=sems_s.at[d], recv_sem=sems_r.at[d],
            device_id=(gx + a, gy + b), device_id_type=MESH)

    def each_halo(act, ref, depth, sems_s, sems_r, stacked, receive=False):
        for d, (a, b) in enumerate(DIRECTIONS):
            ok, _ = neighbour(-a, -b) if receive else neighbour(a, b)

            @pl.when(ok)
            def _():
                act(send_halo(ref, d, depth, sems_s, sems_r, stacked))

    def deep_conduct(d):
        a, b = DIRECTIONS[d]
        ys, yd = y_range(b)
        if a > 0:
            zs, zd = pl.ds(HALO, PLANES - 1), pl.ds(0, HALO - 1)
        else:
            zs, zd = pl.ds(HALO + 1, PLANES - 1), pl.ds(HALO + PLANES + 1, HALO - 1)
        return pltpu.make_async_remote_copy(
            src_ref=fields.at[2, zs, ys, :], dst_ref=fields.at[2, zd, yd, :],
            send_sem=s_cond.at[d], recv_sem=r_cond.at[d],
            device_id=(gx + a, gy + b), device_id_type=MESH)

    def each_deep(act, receive=False):
        for d, (a, b) in enumerate(DIRECTIONS):
            if a == 0:
                continue
            ok, _ = neighbour(-a, -b) if receive else neighbour(a, b)

            @pl.when(ok)
            def _():
                act(deep_conduct(d))

    def start(copy):
        copy.start()

    def wait_recv(copy):
        copy.wait_recv()

    def wait_send(copy):
        copy.wait_send()

    def scatter_rows(stage, rows_ref, n):
        def one(t, _):
            to_gx, to_gy = owner(gy * ROWS + t)
            mine = (to_gx == gx) & (to_gy == gy)

            @pl.when(mine)
            def _():
                pltpu.make_async_copy(stage.at[t], rows_ref.at[1 + gx], s_local.at[n]).start()

            @pl.when(jnp.logical_not(mine))
            def _():
                pltpu.make_async_remote_copy(
                    src_ref=stage.at[t], dst_ref=rows_ref.at[1 + gx],
                    send_sem=s_rows.at[n], recv_sem=r_rows.at[n],
                    device_id=(to_gx, to_gy), device_id_type=MESH).start()
            return 0

        lax.fori_loop(0, ROWS, one, 0)

    def wait_rows(stage, rows_ref, n):
        @pl.when(own_gy == gy)
        def _():
            pltpu.make_async_copy(stage.at[0], rows_ref.at[1], s_local.at[n]).wait()
            part_ref = rows_ref.at[pl.ds(1, TILES - 1)]
            pltpu.make_async_copy(part_ref, part_ref, r_rows.at[n]).wait()

        @pl.when(own_gy != gy)
        def _():
            part_ref = rows_ref.at[pl.ds(1, TILES)]
            pltpu.make_async_copy(part_ref, part_ref, r_rows.at[n]).wait()

    def wait_rows_sent(stage, n):
        @pl.when(own_gy == gy)
        def _():
            part_ref = stage.at[pl.ds(0, ROWS - 1)]
            pltpu.make_async_copy(part_ref, part_ref, s_rows.at[n]).wait()

        @pl.when(own_gy != gy)
        def _():
            pltpu.make_async_copy(stage, stage, s_rows.at[n]).wait()

    def send_back(k):
        def one(i, _):
            mine = (i == gx) & (own_gy == gy)

            @pl.when(mine)
            def _():
                pltpu.make_async_copy(lines.at[k, 1 + i], back.at[k, own_t], s_local.at[2 + k]).start()

            @pl.when(jnp.logical_not(mine))
            def _():
                pltpu.make_async_remote_copy(
                    src_ref=lines.at[k, 1 + i], dst_ref=back.at[k, own_t],
                    send_sem=s_back.at[k], recv_sem=r_back.at[k],
                    device_id=(i, own_gy), device_id_type=MESH).start()
            return 0

        lax.fori_loop(0, GX, one, 0)

    def wait_back(k):
        @pl.when(own_gy == gy)
        def _():
            pltpu.make_async_copy(lines.at[k, 1], back.at[k, 0], s_local.at[2 + k]).wait()
            got = back.at[k, pl.ds(0, ROWS - 1)]
            pltpu.make_async_copy(got, got, r_back.at[k]).wait()
            sent = lines.at[k, pl.ds(1, TILES - 1)]
            pltpu.make_async_copy(sent, sent, s_back.at[k]).wait()

        @pl.when(own_gy != gy)
        def _():
            pltpu.make_async_copy(back.at[k], back.at[k], r_back.at[k]).wait()
            sent = lines.at[k, pl.ds(1, TILES)]
            pltpu.make_async_copy(sent, sent, s_back.at[k]).wait()

    inner = pl.ds(1, TILES)

    def edge(src, dst, n, side):
        to_gx, to_gy = owner(row + (1 if side == 0 else -1))
        return pltpu.make_async_remote_copy(
            src_ref=src.at[inner], dst_ref=dst.at[inner],
            send_sem=s_edge.at[n, side], recv_sem=r_edge.at[n, side],
            device_id=(to_gx, to_gy), device_id_type=MESH)

    has_next, has_prev = row < WHOLE_Y - 1, row > 0

    def edges_start(src, prev, nxt, n):
        @pl.when(has_next)
        def _():
            edge(src, prev, n, 0).start()

        @pl.when(has_prev)
        def _():
            edge(src, nxt, n, 1).start()

    def edges_wait(src, prev, nxt, n):
        @pl.when(has_prev)
        def _():
            edge(src, prev, n, 0).wait_recv()

        @pl.when(has_next)
        def _():
            edge(src, nxt, n, 1).wait_recv()

    def edges_sent(src, prev, nxt, n):
        @pl.when(has_next)
        def _():
            edge(src, prev, n, 0).wait_send()

        @pl.when(has_prev)
        def _():
            edge(src, nxt, n, 1).wait_send()

    own_y = pl.ds(HALO, ROWS)
    mask = tissue[...].astype(jnp.float32)
    v = volt[...]
    conduct = mask * gain[...]
    own = (pl.ds(HALO, PLANES), own_y, slice(None))
    fields[0, *own] = v + pot[...]
    fields[1, *own] = pot[...]
    fields[2, *own] = conduct
    met = (gx >= 0) & (own_gy == gy)
    pl.semaphore_wait(barrier, 104 - 2 * met.astype(jnp.int32))
    each_halo(start, fields, 1, s_fields, r_fields, True)
    each_deep(start)
    ionic_own[...] = mask * v * (v - onset_level) * (v - 1.0)

    for d, (a, b) in enumerate(DIRECTIONS):
        ok, _ = neighbour(-a, -b)

        @pl.when(jnp.logical_not(ok))
        def _():
            zd = z_range(a, HALO)[1]
            yd = y_range(b)[1]
            shape = (zd.size, yd.size, COLS)
            for n in range(3):
                fields[n, zd, yd, :] = jnp.zeros(shape, jnp.float32)
            resid[zd, yd, :] = jnp.zeros(shape, jnp.float32)
    stage_cond[...] = jnp.swapaxes(conduct, 0, 1)
    tile = jnp.zeros((8, COLS), jnp.float32)
    for ref in (row_cond, row_res, cond_prev, cond_next):
        ref[0] = tile
        ref[TILES + 1] = tile
    for k in range(BASIS):
        for ref in (lines, line_prev, line_next):
            ref[k, 0] = tile
            ref[k, TILES + 1] = tile
    blank = jnp.zeros((TILES, 8, COLS), jnp.float32)

    @pl.when(jnp.logical_not(has_prev))
    def _():
        cond_prev[pl.ds(1, TILES)] = blank
        for k in range(BASIS):
            line_prev[k, pl.ds(1, TILES)] = blank

    @pl.when(jnp.logical_not(has_next))
    def _():
        cond_next[pl.ds(1, TILES)] = blank
        for k in range(BASIS):
            line_next[k, pl.ds(1, TILES)] = blank
    part[...] = jnp.zeros_like(part)

    whole = lax.dot_general(
        factor[...], factor[...], (((0,), (0,)), ((), ())), precision=HIGHEST,
        preferred_element_type=jnp.float32)
    in_sum = k_in[0]
    ex_sum = k_ex[0]
    for n in range(1, 9):
        in_sum = in_sum + k_in[n]
        ex_sum = ex_sum + k_ex[n]
    reach = jnp.max(jnp.sum(jnp.abs(whole), axis=1, keepdims=True), axis=0, keepdims=True)
    bound = reach * (4.0 * gain_top * in_sum + 4.0 * ex_sum)
    matrix[...] = whole * (1.0 / bound)
    eye = lax.broadcasted_iota(jnp.int32, whole.shape, 0) == lax.broadcasted_iota(jnp.int32, whole.shape, 1)
    mean = jnp.sum(jnp.sum(jnp.where(eye, whole, 0.0), axis=1, keepdims=True), axis=0, keepdims=True) / WHOLE_Z
    shift = SHIFT * mean * (2.0 * in_sum + 2.0 * ex_sum) / bound

    top = 1.0 + time_step * 4.0 * gain_top * in_sum
    ones = jnp.ones((1, COLS), jnp.float32)
    top = ones * top
    centre = (top + 1.0) / 2.0
    half = (top - 1.0) / 2.0
    ratio = centre / half
    weight = 1.0 / ratio

    each_halo(wait_recv, fields, 1, s_fields, r_fields, True, receive=True)

    def first_plane(z, _):
        s = stencil(fields[2, z - 1], fields[2, z], fields[2, z + 1], k_in, first, last)
        diag[z] = s
        w = [fields[2, z + n] * fields[0, z + n] for n in (-1, 0, 1)]
        c = fields[2, z]
        ki = c * (s * fields[0, z] - stencil(*w, k_in, first, last))
        r = -ionic_rate * ionic_own[z - HALO] - time_step * ki[HALO : HALO + ROWS]
        resid[z, own_y, :] = r
        return 0

    lax.fori_loop(HALO, HALO + PLANES, first_plane, 0)
    each_halo(start, resid, HALO, s_resid, r_resid, False)

    each_deep(wait_recv, receive=True)

    def diag_plane(z, _):
        diag[z] = stencil(fields[2, z - 1], fields[2, z], fields[2, z + 1], k_in, first, last)
        return 0

    lax.fori_loop(1, HALO, diag_plane, 0)
    lax.fori_loop(HALO + PLANES, EXT_Z - 1, diag_plane, 0)
    each_halo(wait_recv, resid, HALO, s_resid, r_resid, False, receive=True)

    scatter_rows(stage_cond, row_cond, 0)

    inv_centre = 1.0 / centre

    def first_update(z, _):
        upd[0, z] = resid[z] * inv_centre
        return 0

    lax.fori_loop(0, EXT_Z, first_update, 0)

    def add_update(slot):
        def one(z, _):
            fields[0, z] = fields[0, z] + upd[slot, z]
            return 0

        lax.fori_loop(HALO - 1, HALO + PLANES + 1, one, 0)
        new_volt[...] = new_volt[...] + upd[slot, pl.ds(HALO, PLANES), own_y, :]

    each_halo(wait_send, fields, 1, s_fields, r_fields, True)
    new_volt[...] = volt[...]
    add_update(0)

    def sweep(n, weight):
        old = lax.rem(n + 1, 2)
        new = lax.rem(n, 2)
        weight_next = 1.0 / (2.0 * ratio - weight)
        keep = weight_next * weight
        gain_r = 2.0 * weight_next / half

        def one(z, _):
            w = [fields[2, z + m] * upd[old, z + m] for m in (-1, 0, 1)]
            u = upd[old, z]
            c = fields[2, z]
            ki = c * (diag[z] * u - stencil(*w, k_in, first, last))
            r = resid[z] - (u + time_step * ki)
            resid[z] = r
            upd[new, z] = keep * u + gain_r * r
            return 0

        lax.fori_loop(n, EXT_Z - n, one, 0)
        add_update(new)
        return weight_next

    each_halo(wait_send, resid, HALO, s_resid, r_resid, False)
    lax.fori_loop(1, CHEB, sweep, weight)

    ex_total = 2.0 * ex_sum

    def elliptic_plane(z, _):
        c = fields[2, z]
        w = [fields[2, z + m] * fields[0, z + m] for m in (-1, 0, 1)]
        ki = c * (diag[z] * fields[0, z] - stencil(*w, k_in, first, last))
        p = [fields[1, z + m] for m in (-1, 0, 1)]
        ke = ex_total * p[1] - stencil(*p, k_ex, first, last)
        upd[0, z] = -ki - ke
        return 0

    lax.fori_loop(HALO, HALO + PLANES, elliptic_plane, 0)
    stage_res[...] = jnp.swapaxes(upd[0, pl.ds(HALO, PLANES), own_y, :], 0, 1)
    scatter_rows(stage_res, row_res, 1)

    wait_rows(stage_cond, row_cond, 0)
    edges_start(row_cond, cond_prev, cond_next, BASIS)
    wait_rows(stage_res, row_res, 1)

    def apply_matrix(src, k, shift=None):
        out = jnp.dot(matrix[...], src.reshape(WHOLE_Z, COLS), precision=HIGHEST,
                      preferred_element_type=jnp.float32)
        out = out.reshape(TILES, 8, COLS)
        if shift is not None:
            out = out - shift * lines[k - 1, inner]
        lines[k, inner] = out

    def product(e, a, b):
        total = jnp.sum(a * b, axis=0)
        part[pl.ds(e, 1), :] = jnp.sum(total, axis=0, keepdims=True)

    CHUNK = 8

    def chunk(ref, at):
        return ref[pl.ds(at, CHUNK + 2)].reshape((CHUNK + 2) * 8, COLS)

    def put(ref, at, value):
        ref[pl.ds(at, CHUNK)] = value[8 : 8 + CHUNK * 8].reshape(CHUNK, 8, COLS)

    def operate(k):
        def one(i, _):
            at = i * CHUNK
            c = [chunk(r, at) for r in (cond_prev, row_cond, cond_next)]
            s = [chunk(r, at) for r in (line_prev.at[k], lines.at[k], line_next.at[k])]
            w = [a * b for a, b in zip(c, s)]
            ki = c[1] * (chunk(row_diag, at) * s[1] - stencil(*w, k_in, first, last, True))
            ke = ex_total * s[1] - stencil(*s, k_ex, first, last, True)
            put(image.at[k], at, ki + ke)
            return 0

        lax.fori_loop(0, TILES // CHUNK, one, 0)

    def line_diag(i, _):
        at = i * CHUNK
        c = [chunk(r, at) for r in (cond_prev, row_cond, cond_next)]
        row_diag[pl.ds(at + 1, CHUNK)] = stencil(*c, k_in, first, last, True)[8 : 8 + CHUNK * 8].reshape(
            CHUNK, 8, COLS)
        return 0

    apply_matrix(row_res[inner], 0)
    edges_start(lines.at[0], line_prev.at[0], line_next.at[0], 0)
    send_back(0)
    product(0, lines[0, inner], row_res[inner])
    edges_wait(row_cond, cond_prev, cond_next, BASIS)
    row_diag[0] = tile
    row_diag[TILES + 1] = tile
    lax.fori_loop(0, TILES // CHUNK, line_diag, 0)

    at = BASIS
    for k in range(BASIS):
        edges_wait(lines.at[k], line_prev.at[k], line_next.at[k], k)
        operate(k)
        if k < BASIS - 1:
            apply_matrix(image[k], k + 1, shift)
            edges_start(lines.at[k + 1], line_prev.at[k + 1], line_next.at[k + 1], k + 1)
            send_back(k + 1)
            product(k + 1, lines[k + 1, inner], row_res[inner])
            for m in range(k + 1):
                product(at, lines[m, inner], image[k])
                at += 1
        else:
            for m in range(k):
                product(at, lines[k, inner], image[m])
                at += 1
            product(at, lines[k, inner], image[k])

    def sum_over(buf, n, me, peer):
        buf[me] = part[...]

        def one(d, _):
            to = lax.rem(me + d, 16)
            pltpu.make_async_remote_copy(
                src_ref=part, dst_ref=buf.at[me], send_sem=s_sum.at[n], recv_sem=r_sum.at[n],
                device_id=peer(to), device_id_type=MESH).start()
            return 0

        lax.fori_loop(1, 16, one, 0)
        got = buf.at[pl.ds(0, 15)]
        pltpu.make_async_copy(got, got, r_sum.at[n]).wait()
        pltpu.make_async_copy(got, got, s_sum.at[n]).wait()
        part[...] = jnp.sum(buf[...], axis=0)

    sum_over(gather_a, 0, me_a, peer_a)
    sum_over(gather_b, 1, me_b, peer_b)

    totals = jnp.broadcast_to(jnp.sum(part[...], axis=1, keepdims=True), (16, COLS))
    value = [totals[e : e + 1] for e in range(14)]
    rhs = value[:BASIS]
    gram = {}
    at = BASIS
    for k in range(BASIS - 1):
        for m in range(k + 1):
            gram[m, k] = value[at]
            at += 1
    for m in range(BASIS):
        gram[m, BASIS - 1] = value[at]
        at += 1

    low, pivot = {}, {}
    for j in range(BASIS):
        d = gram[j, j]
        for m in range(j):
            d = d - low[j, m] * low[j, m] * pivot[m]
        pivot[j] = d
        for i in range(j + 1, BASIS):
            e = gram[j, i]
            for m in range(j):
                e = e - low[i, m] * low[j, m] * pivot[m]
            low[i, j] = e / d
    sol = list(rhs)
    for i in range(BASIS):
        for m in range(i):
            sol[i] = sol[i] - low[i, m] * sol[m]
    sol = [a / pivot[i] for i, a in enumerate(sol)]
    for i in reversed(range(BASIS)):
        for m in range(i + 1, BASIS):
            sol[i] = sol[i] - low[m, i] * sol[m]

    for k in range(BASIS):
        wait_back(k)
    total = sol[0] * back[0]
    for k in range(1, BASIS):
        total = total + sol[k] * back[k]
    new_pot[...] = pot[...] + jnp.swapaxes(total, 0, 1)

    each_deep(wait_send)
    wait_rows_sent(stage_cond, 0)
    wait_rows_sent(stage_res, 1)
    edges_sent(row_cond, cond_prev, cond_next, BASIS)
    for k in range(BASIS):
        edges_sent(lines.at[k], line_prev.at[k], line_next.at[k], k)


def body(voltage, potential, tissue, gain, couplings, line_factor):
    f32 = jnp.float32
    block = jax.ShapeDtypeStruct((PLANES, ROWS, COLS), f32)
    vmem = pl.BlockSpec(memory_space=pltpu.VMEM)
    line = (TILES + 2, 8, COLS)
    dma = pltpu.SemaphoreType.DMA
    return pl.pallas_call(
        kernel,
        name="bidomain",
        out_shape=(block, block),
        in_specs=[pl.BlockSpec(memory_space=pltpu.SMEM)] + [pl.BlockSpec(memory_space=pl.ANY)] * 5,
        out_specs=(vmem, vmem),
        scratch_shapes=[
            pltpu.VMEM((PLANES, ROWS, COLS), f32),
            pltpu.VMEM((PLANES, ROWS, COLS), f32),
            pltpu.VMEM((PLANES, ROWS, COLS), jnp.int32),
            pltpu.VMEM((PLANES, ROWS, COLS), f32),
            pltpu.VMEM((WHOLE_Z, WHOLE_Z), f32),
            pltpu.VMEM((3, EXT_Z, EXT_Y, COLS), f32),
            pltpu.VMEM((EXT_Z, EXT_Y, COLS), f32),
            pltpu.VMEM((2, EXT_Z, EXT_Y, COLS), f32),
            pltpu.VMEM((EXT_Z, EXT_Y, COLS), f32),
            pltpu.VMEM((PLANES, ROWS, COLS), f32),
            pltpu.VMEM((WHOLE_Z, WHOLE_Z), f32),
            pltpu.VMEM((ROWS, PLANES, COLS), f32),
            pltpu.VMEM((ROWS, PLANES, COLS), f32),
            pltpu.VMEM((ROWS, PLANES, COLS), f32),
            pltpu.VMEM(line, f32),
            pltpu.VMEM(line, f32),
            pltpu.VMEM((BASIS, *line), f32),
            pltpu.VMEM((BASIS, *line), f32),
            pltpu.VMEM((BASIS, *line), f32),
            pltpu.VMEM(line, f32),
            pltpu.VMEM(line, f32),
            pltpu.VMEM((BASIS, TILES, 8, COLS), f32),
            pltpu.VMEM(line, f32),
            pltpu.VMEM((BASIS, ROWS, PLANES, COLS), f32),
            pltpu.VMEM((16, COLS), f32),
            pltpu.VMEM((16, 16, COLS), f32),
            pltpu.VMEM((16, 16, COLS), f32),
            dma((8,)), dma((8,)), dma((8,)), dma((8,)), dma((8,)), dma((8,)),
            dma((2,)), dma((2,)), dma((BASIS + 1, 2)), dma((BASIS + 1, 2)),
            dma((BASIS,)), dma((BASIS,)), dma((2,)), dma((2,)), dma((2 + BASIS,)), dma((5,)),
        ],
        compiler_params=pltpu.CompilerParams(
            collective_id=0, has_side_effects=True, vmem_limit_bytes=48 * 2**20),
    )(couplings, voltage, potential, tissue, gain, line_factor)


def solution(mesh):
    block = P("gx", "gy", None)
    return jax.shard_map(
        body, mesh=mesh, in_specs=(block, block, block, block, P(), P()),
        out_specs=(block, block), check_vma=False)
```

time: 650 us -> 105 us (0.16)
  blocking collectives: 230 us -> 0 us
  starting transfers between devices: 195 us -> 0 us
  other arithmetic: 121 us -> 0 us
  Pallas kernels: 0 us -> 98 us
  waiting for transfers between devices: 69.5 us -> 0 us
  between operations: 18.5 us -> 0.65 us
    ppermute x64 -> x0, starting transfers between devices: 195 us -> none  [the longest x32 139 us: extended(): lax.ppermute(tail, axis, [(i, (i + 1) % count) for i in range(ends)])]
    psum x20 -> x0, blocking collectives: 158 us -> none  [by_axis(): return functools.reduce(lax.psum, axes, array)]
    pallas_call x0 -> x1, Pallas kernels: none -> 98 us  [body(): pl.pallas_call(kernel, name='bidomain', out_shape=(block, block), in_spec...]
    all_to_all x2 -> x0, blocking collectives: 71.7 us -> none  [the longest x1 52.1 us: side_by_side(): lax.all_to_all(both, axis, split_axis=split_dim, concat_axis=concat_dim,...]
    ppermute x64 -> x0, waiting for transfers between devices: 69.5 us -> none  [the longest x32 66.9 us: extended(): lax.ppermute(head, axis, [((i + 1) % count, i) for i in range(ends)])]
    reduce_sum x5 -> x0, other arithmetic: 51.1 us -> none  [the longest x4 50.5 us: joint_products(): jnp.sum(third * second)]
    add x7 -> x0, other arithmetic: 44.4 us -> none  [the longest x6 38.1 us: body(): weight_next * weight_now * update]
    sub x4 -> x0, other arithmetic: 12.5 us -> none  [the longest x1 12.4 us: body(): residual = -est_intra - (pot_intra + pot_extra)]
  transfers between devices with their start and end apart: 64 -> 0, of which waited for: 24 -> 0; matrix products, arithmetic and copies ran while one was open for 1% -> 0% of each run, Pallas kernels for 0% -> 0%
where the time goes in v1:
time: 105 us
  Pallas kernels  98 us (93%)
  local copies, waits for them, and re-layouts  6.55 us (6%)
    pallas_call x1, Pallas kernels, body(): pl.pallas_call(kernel, name='bidomain', out_shape=(block, block), in_spec...  98 us
    unnamed x14, local copies, waits for them, and re-layouts  6.55 us

profile of v1, /device:TPU:1, one launch (start us, length us, event | category | flops | bytes accessed | tf_op | source)
XLA Modules:
  0.0 105.2 jit_solution(13181430976654098867)
XLA Ops:
  0.6 0.0 copy-start
  0.6 0.9 copy-done
  1.6 0.0 copy-start.1
  1.6 0.9 copy-done.1
  2.5 0.0 copy-start.2
  2.5 0.9 copy-done.2
  3.4 0.0 copy-start.3
  3.4 0.9 copy-done.3
  4.3 0.0 copy-start.4
  4.3 0.9 copy-done.4
  5.2 0.0 copy-start.5
  5.2 0.7 copy-done.5
  5.9 98.0 %bidomain.1 = (f32[8,32,128]{2,1,0:T(8,128)S(1)}, f32[8,32,128]{2,1,0:T(8,128)S(1)}) custom-call(f32[2,9]{1,0:T(2,128)S(1)} %copy-done.5, f32[8,32,128]{2,1,0:T(8,128)S(1)} %copy-done.1, f32[8,32,128]{2,1,0:T(8,128)S(1)} %copy-done.2, s32[8,32,128]{2,1,0:T(8,128)S(1)} %copy-done.3, f32[8,32,128]{2,1,0:T(8,128)S(1)} %copy-done.4, f32[256,256]{1,0:T(8,128)S(1)} %copy-done), custom_call_target="tpu_custom_call" | custom-call | tf_op jit(solution)/shard_map/bidomain/pallas_call | solution.py:621
  103.9 0.7 copy.10
  104.6 0.7 copy.11
Async XLA Ops:
  0.6 1.0 copy-start
  1.6 0.9 copy-start.1
  2.5 0.9 copy-start.2
  3.4 0.9 copy-start.3
  4.3 0.9 copy-start.4
  5.2 0.7 copy-start.5

commit v2 on v1

--- a/solution.py
+++ b/solution.py
@@ -85,57 +85,40 @@
 def kernel(
     coup, volt_in, pot_in, tissue_in, gain_in, factor_in, new_volt, new_pot,
     volt, pot, tissue, gain, factor,
-    fields, resid, upd, diag, ionic_own, matrix,
-    stage_cond, stage_res, stage_row,
+    fields, resid, upd, diag, estimate, own_term, matrix,
+    stage_cond, stage_res,
     row_cond, row_res, lines, line_prev, line_next, cond_prev, cond_next,
     image, row_diag, back, part, gather_a, gather_b,
-    s_fields, r_fields, s_cond, r_cond, s_resid, r_resid,
-    s_rows, r_rows, s_edge, r_edge, s_back, r_back, s_sum, r_sum, s_local, s_take,
+    s_fields, r_fields, s_cond, r_cond, s_pot, r_pot, s_resid, r_resid,
+    s_rows, r_rows, s_edge, r_edge, s_back, r_back, s_sum, r_sum, s_take, far,
 ):
     gx = lax.axis_index("gx")
     gy = lax.axis_index("gy")
     row = own_row(gx, gy)
     own_gy = row // ROWS
     own_t = row % ROWS
-    me_a = ((gx % 8) // 2) * 4 + gy // 2
-    me_b = (gx // 8) * 4 + (gy % 2) * 2 + gx % 2
-
-    def peer_a(p):
-        return (gx // 8) * 8 + (p // 4) * 2 + gx % 2, (p % 4) * 2 + gy % 2
-
-    def peer_b(p):
-        return (p // 4) * 8 + ((gx % 8) // 2) * 2 + p % 2, (gy // 2) * 2 + (p % 4) // 2
+    chip_z = (gx // 8) * 2 + gy % 2
+    chip_y = gy // 2
+    spot = gx % 8
+
+    def at_z(z):
+        return (z // 2) * 8 + spot, chip_y * 2 + z % 2
+
+    def at_y(y):
+        return gx, y * 2 + gy % 2
 
     barrier = pltpu.get_barrier_semaphore()
 
-    def greet(to):
-        pl.semaphore_signal(barrier, inc=1, device_id=to, device_id_type=MESH)
+    def greet(sem, to):
+        pl.semaphore_signal(sem, inc=1, device_id=to, device_id_type=MESH)
 
     for a, b in DIRECTIONS:
-        greet((lax.rem(gx + a + GX, GX), lax.rem(gy + b + GY, GY)))
-    greet(owner(lax.rem(row + 1, WHOLE_Y)))
-    greet(owner(lax.rem(row + WHOLE_Y - 1, WHOLE_Y)))
-
-    def greet_sixteen(d, _):
-        greet(peer_a(lax.rem(me_a + d, 16)))
-        greet(peer_b(lax.rem(me_b + d, 16)))
-        return 0
-
-    lax.fori_loop(1, 16, greet_sixteen, 0)
-
-    def greet_rows(t, _):
-        to_gx, to_gy = owner(gy * ROWS + t)
-
-        @pl.when(jnp.logical_not((to_gx == gx) & (to_gy == gy)))
-        def _():
-            greet((to_gx, to_gy))
-
-        @pl.when(jnp.logical_not((t == gx) & (own_gy == gy)))
-        def _():
-            greet((t, own_gy))
-        return 0
-
-    lax.fori_loop(0, ROWS, greet_rows, 0)
+        greet(barrier, (lax.rem(gx + a + GX, GX), lax.rem(gy + b + GY, GY)))
+    for d in range(1, 8):
+        greet(barrier, at_z(lax.rem(chip_z + d, 8)))
+        greet(barrier, ((gx // 8) * 8 + lax.rem(spot + d, 8), gy))
+    for d in range(1, 4):
+        greet(barrier, at_y(lax.rem(chip_y + d, 4)))
     takes = [
         pltpu.make_async_copy(src, dst, s_take.at[n])
         for n, (src, dst) in enumerate(
@@ -181,7 +164,7 @@
         else:
             zs, zd = pl.ds(HALO + 1, PLANES - 1), pl.ds(HALO + PLANES + 1, HALO - 1)
         return pltpu.make_async_remote_copy(
-            src_ref=fields.at[2, zs, ys, :], dst_ref=fields.at[2, zd, yd, :],
+            src_ref=fields.at[1, zs, ys, :], dst_ref=fields.at[1, zd, yd, :],
             send_sem=s_cond.at[d], recv_sem=r_cond.at[d],
             device_id=(gx + a, gy + b), device_id_type=MESH)
 
@@ -204,16 +187,13 @@
     def wait_send(copy):
         copy.wait_send()
 
+    own_group = own_gy == gy
+
     def scatter_rows(stage, rows_ref, n):
         def one(t, _):
             to_gx, to_gy = owner(gy * ROWS + t)
-            mine = (to_gx == gx) & (to_gy == gy)
-
-            @pl.when(mine)
-            def _():
-                pltpu.make_async_copy(stage.at[t], rows_ref.at[1 + gx], s_local.at[n]).start()
-
-            @pl.when(jnp.logical_not(mine))
+
+            @pl.when((to_gx != gx) | (to_gy != gy))
             def _():
                 pltpu.make_async_remote_copy(
                     src_ref=stage.at[t], dst_ref=rows_ref.at[1 + gx],
@@ -221,62 +201,66 @@
                     device_id=(to_gx, to_gy), device_id_type=MESH).start()
             return 0
 
-        lax.fori_loop(0, ROWS, one, 0)
+        lax.fori_loop(0, ROWS, one, 0, unroll=4)
+
+        @pl.when(own_group)
+        def _():
+            rows_ref[1 + gx] = stage[own_t]
 
     def wait_rows(stage, rows_ref, n):
-        @pl.when(own_gy == gy)
-        def _():
-            pltpu.make_async_copy(stage.at[0], rows_ref.at[1], s_local.at[n]).wait()
+        @pl.when(own_group)
+        def _():
             part_ref = rows_ref.at[pl.ds(1, TILES - 1)]
             pltpu.make_async_copy(part_ref, part_ref, r_rows.at[n]).wait()
 
-        @pl.when(own_gy != gy)
+        @pl.when(jnp.logical_not(own_group))
         def _():
             part_ref = rows_ref.at[pl.ds(1, TILES)]
             pltpu.make_async_copy(part_ref, part_ref, r_rows.at[n]).wait()
 
     def wait_rows_sent(stage, n):
-        @pl.when(own_gy == gy)
+        @pl.when(own_group)
         def _():
             part_ref = stage.at[pl.ds(0, ROWS - 1)]
             pltpu.make_async_copy(part_ref, part_ref, s_rows.at[n]).wait()
 
-        @pl.when(own_gy != gy)
+        @pl.when(jnp.logical_not(own_group))
         def _():
             pltpu.make_async_copy(stage, stage, s_rows.at[n]).wait()
 
-    def send_back(k):
+    def send_back(n):
+        two = pl.ds(2 * n, 2)
+
         def one(i, _):
-            mine = (i == gx) & (own_gy == gy)
-
-            @pl.when(mine)
-            def _():
-                pltpu.make_async_copy(lines.at[k, 1 + i], back.at[k, own_t], s_local.at[2 + k]).start()
-
-            @pl.when(jnp.logical_not(mine))
+            @pl.when((i != gx) | (own_gy != gy))
             def _():
                 pltpu.make_async_remote_copy(
-                    src_ref=lines.at[k, 1 + i], dst_ref=back.at[k, own_t],
-                    send_sem=s_back.at[k], recv_sem=r_back.at[k],
+                    src_ref=lines.at[two, 1 + i], dst_ref=back.at[two, own_t],
+                    send_sem=s_back.at[n], recv_sem=r_back.at[n],
                     device_id=(i, own_gy), device_id_type=MESH).start()
             return 0
 
-        lax.fori_loop(0, GX, one, 0)
-
-    def wait_back(k):
-        @pl.when(own_gy == gy)
-        def _():
-            pltpu.make_async_copy(lines.at[k, 1], back.at[k, 0], s_local.at[2 + k]).wait()
-            got = back.at[k, pl.ds(0, ROWS - 1)]
-            pltpu.make_async_copy(got, got, r_back.at[k]).wait()
-            sent = lines.at[k, pl.ds(1, TILES - 1)]
-            pltpu.make_async_copy(sent, sent, s_back.at[k]).wait()
-
-        @pl.when(own_gy != gy)
-        def _():
-            pltpu.make_async_copy(back.at[k], back.at[k], r_back.at[k]).wait()
-            sent = lines.at[k, pl.ds(1, TILES)]
-            pltpu.make_async_copy(sent, sent, s_back.at[k]).wait()
+        lax.fori_loop(0, GX, one, 0, unroll=4)
+
+        @pl.when(own_group)
+        def _():
+            for k in (2 * n, 2 * n + 1):
+                back[k, own_t] = lines[k, 1 + gx]
+
+    def wait_back(n):
+        two = pl.ds(2 * n, 2)
+
+        @pl.when(own_group)
+        def _():
+            got = back.at[two, pl.ds(0, ROWS - 1)]
+            pltpu.make_async_copy(got, got, r_back.at[n]).wait()
+            pltpu.make_async_copy(got, got, s_back.at[n]).wait()
+
+        @pl.when(jnp.logical_not(own_group))
+        def _():
+            got = back.at[two]
+            pltpu.make_async_copy(got, got, r_back.at[n]).wait()
+            pltpu.make_async_copy(got, got, s_back.at[n]).wait()
 
     inner = pl.ds(1, TILES)
 
@@ -317,18 +301,23 @@
             edge(src, nxt, n, 1).wait_send()
 
     own_y = pl.ds(HALO, ROWS)
-    mask = tissue[...].astype(jnp.float32)
+    conduct = tissue[...].astype(jnp.float32) * gain[...]
+    own = (pl.ds(HALO, PLANES), own_y, slice(None))
+    fields[0, *own] = volt[...] + pot[...]
+    fields[1, *own] = conduct
+    fields[2, *own] = pot[...]
+    pl.semaphore_wait(barrier, 25)
+    near = fields.at[pl.ds(0, 2)]
+    each_halo(start, near, 1, s_fields, r_fields, True)
+    each_deep(start)
+    each_halo(start, fields.at[2], 1, s_pot, r_pot, False)
+    for d in range(1, 8):
+        greet(far, at_z(lax.rem(chip_z + d, 8)))
+    for d in range(1, 4):
+        greet(far, at_y(lax.rem(chip_y + d, 4)))
     v = volt[...]
-    conduct = mask * gain[...]
-    own = (pl.ds(HALO, PLANES), own_y, slice(None))
-    fields[0, *own] = v + pot[...]
-    fields[1, *own] = pot[...]
-    fields[2, *own] = conduct
-    met = (gx >= 0) & (own_gy == gy)
-    pl.semaphore_wait(barrier, 104 - 2 * met.astype(jnp.int32))
-    each_halo(start, fields, 1, s_fields, r_fields, True)
-    each_deep(start)
-    ionic_own[...] = mask * v * (v - onset_level) * (v - 1.0)
+    ionic = tissue[...].astype(jnp.float32) * v * (v - onset_level) * (v - 1.0)
+    own_term[...] = -ionic_rate * ionic
 
     for d, (a, b) in enumerate(DIRECTIONS):
         ok, _ = neighbour(-a, -b)
@@ -363,7 +352,6 @@
         cond_next[pl.ds(1, TILES)] = blank
         for k in range(BASIS):
             line_next[k, pl.ds(1, TILES)] = blank
-    part[...] = jnp.zeros_like(part)
 
     whole = lax.dot_general(
         factor[...], factor[...], (((0,), (0,)), ((), ())), precision=HIGHEST,
@@ -388,16 +376,14 @@
     ratio = centre / half
     weight = 1.0 / ratio
 
-    each_halo(wait_recv, fields, 1, s_fields, r_fields, True, receive=True)
+    each_halo(wait_recv, near, 1, s_fields, r_fields, True, receive=True)
 
     def first_plane(z, _):
-        s = stencil(fields[2, z - 1], fields[2, z], fields[2, z + 1], k_in, first, last)
+        s = stencil(fields[1, z - 1], fields[1, z], fields[1, z + 1], k_in, first, last)
         diag[z] = s
-        w = [fields[2, z + n] * fields[0, z + n] for n in (-1, 0, 1)]
-        c = fields[2, z]
-        ki = c * (s * fields[0, z] - stencil(*w, k_in, first, last))
-        r = -ionic_rate * ionic_own[z - HALO] - time_step * ki[HALO : HALO + ROWS]
-        resid[z, own_y, :] = r
+        w = [fields[1, z + n] * fields[0, z + n] for n in (-1, 0, 1)]
+        ki = fields[1, z] * (s * fields[0, z] - stencil(*w, k_in, first, last))
+        resid[z, own_y, :] = own_term[z - HALO] - time_step * ki[HALO : HALO + ROWS]
         return 0
 
     lax.fori_loop(HALO, HALO + PLANES, first_plane, 0)
@@ -406,11 +392,23 @@
     each_deep(wait_recv, receive=True)
 
     def diag_plane(z, _):
-        diag[z] = stencil(fields[2, z - 1], fields[2, z], fields[2, z + 1], k_in, first, last)
+        diag[z] = stencil(fields[1, z - 1], fields[1, z], fields[1, z + 1], k_in, first, last)
         return 0
 
     lax.fori_loop(1, HALO, diag_plane, 0)
     lax.fori_loop(HALO + PLANES, EXT_Z - 1, diag_plane, 0)
+    each_halo(wait_recv, fields.at[2], 1, s_pot, r_pot, False, receive=True)
+    ex_total = 2.0 * ex_sum
+
+    def extra_plane(z, _):
+        p = [fields[2, z + m] for m in (-1, 0, 1)]
+        ke = stencil(*p, k_ex, first, last) - ex_total * p[1]
+        own_term[z - HALO] = ke[HALO : HALO + ROWS]
+        return 0
+
+    lax.fori_loop(HALO, HALO + PLANES, extra_plane, 0)
+    each_halo(wait_send, near, 1, s_fields, r_fields, True)
+    pl.semaphore_wait(far, 10)
     each_halo(wait_recv, resid, HALO, s_resid, r_resid, False, receive=True)
 
     scatter_rows(stage_cond, row_cond, 0)
@@ -418,22 +416,12 @@
     inv_centre = 1.0 / centre
 
     def first_update(z, _):
-        upd[0, z] = resid[z] * inv_centre
+        u = resid[z] * inv_centre
+        upd[0, z] = u
+        estimate[z] = u
         return 0
 
     lax.fori_loop(0, EXT_Z, first_update, 0)
-
-    def add_update(slot):
-        def one(z, _):
-            fields[0, z] = fields[0, z] + upd[slot, z]
-            return 0
-
-        lax.fori_loop(HALO - 1, HALO + PLANES + 1, one, 0)
-        new_volt[...] = new_volt[...] + upd[slot, pl.ds(HALO, PLANES), own_y, :]
-
-    each_halo(wait_send, fields, 1, s_fields, r_fields, True)
-    new_volt[...] = volt[...]
-    add_update(0)
 
     def sweep(n, weight):
         old = lax.rem(n + 1, 2)
@@ -442,40 +430,46 @@
         keep = weight_next * weight
         gain_r = 2.0 * weight_next / half
 
-        def one(z, _):
-            w = [fields[2, z + m] * upd[old, z + m] for m in (-1, 0, 1)]
-            u = upd[old, z]
-            c = fields[2, z]
-            ki = c * (diag[z] * u - stencil(*w, k_in, first, last))
-            r = resid[z] - (u + time_step * ki)
-            resid[z] = r
-            upd[new, z] = keep * u + gain_r * r
+        def pair(i, _):
+            z = n + 2 * i
+            c = [fields[1, z + m] for m in (-1, 0, 1, 2)]
+            u = [upd[old, z + m] for m in (-1, 0, 1, 2)]
+            w = [a * b for a, b in zip(c, u)]
+            for m in (1, 2):
+                ki = c[m] * (diag[z + m - 1] * u[m] - stencil(*w[m - 1 : m + 2], k_in, first, last))
+                r = resid[z + m - 1] - (u[m] + time_step * ki)
+                resid[z + m - 1] = r
+                fresh = keep * u[m] + gain_r * r
+                upd[new, z + m - 1] = fresh
+                estimate[z + m - 1] = estimate[z + m - 1] + fresh
             return 0
 
-        lax.fori_loop(n, EXT_Z - n, one, 0)
-        add_update(new)
+        lax.fori_loop(0, EXT_Z // 2 - n, pair, 0)
         return weight_next
 
     each_halo(wait_send, resid, HALO, s_resid, r_resid, False)
-    lax.fori_loop(1, CHEB, sweep, weight)
-
-    ex_total = 2.0 * ex_sum
-
-    def elliptic_plane(z, _):
-        c = fields[2, z]
-        w = [fields[2, z + m] * fields[0, z + m] for m in (-1, 0, 1)]
-        ki = c * (diag[z] * fields[0, z] - stencil(*w, k_in, first, last))
-        p = [fields[1, z + m] for m in (-1, 0, 1)]
-        ke = ex_total * p[1] - stencil(*p, k_ex, first, last)
-        upd[0, z] = -ki - ke
-        return 0
-
-    lax.fori_loop(HALO, HALO + PLANES, elliptic_plane, 0)
-    stage_res[...] = jnp.swapaxes(upd[0, pl.ds(HALO, PLANES), own_y, :], 0, 1)
-    scatter_rows(stage_res, row_res, 1)
-
+    weight = lax.fori_loop(1, CHEB - 2, sweep, weight)
     wait_rows(stage_cond, row_cond, 0)
     edges_start(row_cond, cond_prev, cond_next, BASIS)
+    lax.fori_loop(CHEB - 2, CHEB, sweep, weight)
+
+    def total_plane(z, _):
+        fields[0, z] = fields[0, z] + estimate[z]
+        return 0
+
+    lax.fori_loop(HALO - 1, HALO + PLANES + 1, total_plane, 0)
+
+    def elliptic_plane(z, _):
+        w = [fields[1, z + m] * fields[0, z + m] for m in (-1, 0, 1)]
+        ki = fields[1, z] * (diag[z] * fields[0, z] - stencil(*w, k_in, first, last))
+        own_term[z - HALO] = own_term[z - HALO] - ki[HALO : HALO + ROWS]
+        return 0
+
+    lax.fori_loop(HALO, HALO + PLANES, elliptic_plane, 0)
+    stage_res[...] = jnp.swapaxes(own_term[...], 0, 1)
+    scatter_rows(stage_res, row_res, 1)
+
+    new_volt[...] = volt[...] + estimate[pl.ds(HALO, PLANES), own_y, :]
     wait_rows(stage_res, row_res, 1)
 
     def apply_matrix(src, k, shift=None):
@@ -486,9 +480,12 @@
             out = out - shift * lines[k - 1, inner]
         lines[k, inner] = out
 
-    def product(e, a, b):
-        total = jnp.sum(a * b, axis=0)
-        part[pl.ds(e, 1), :] = jnp.sum(total, axis=0, keepdims=True)
+    sums = jnp.zeros((1, COLS), jnp.float32)
+
+    def product(sums, e, a, b):
+        total = jnp.sum((a * b).reshape(4, TILES // 4, 8, COLS), axis=0)
+        total = jnp.sum(jnp.sum(total, axis=0), axis=0, keepdims=True)
+        return sums + jnp.where(lane == e, jnp.sum(total, axis=1, keepdims=True), 0.0)
 
     CHUNK = 8
 
@@ -520,12 +517,11 @@
 
     apply_matrix(row_res[inner], 0)
     edges_start(lines.at[0], line_prev.at[0], line_next.at[0], 0)
-    send_back(0)
-    product(0, lines[0, inner], row_res[inner])
     edges_wait(row_cond, cond_prev, cond_next, BASIS)
     row_diag[0] = tile
     row_diag[TILES + 1] = tile
     lax.fori_loop(0, TILES // CHUNK, line_diag, 0)
+    sums = product(sums, 0, lines[0, inner], row_res[inner])
 
     at = BASIS
     for k in range(BASIS):
@@ -534,48 +530,56 @@
         if k < BASIS - 1:
             apply_matrix(image[k], k + 1, shift)
             edges_start(lines.at[k + 1], line_prev.at[k + 1], line_next.at[k + 1], k + 1)
-            send_back(k + 1)
-            product(k + 1, lines[k + 1, inner], row_res[inner])
+            if k % 2 == 0:
+                send_back(k // 2)
+            sums = product(sums, k + 1, lines[k + 1, inner], row_res[inner])
             for m in range(k + 1):
-                product(at, lines[m, inner], image[k])
+                sums = product(sums, at, lines[m, inner], image[k])
                 at += 1
+            if k == BASIS - 2:
+                for m in range(k + 1):
+                    sums = product(sums, at, lines[k + 1, inner], image[m])
+                    at += 1
         else:
-            for m in range(k):
-                product(at, lines[k, inner], image[m])
-                at += 1
-            product(at, lines[k, inner], image[k])
-
-    def sum_over(buf, n, me, peer):
-        buf[me] = part[...]
-
-        def one(d, _):
-            to = lax.rem(me + d, 16)
+            sums = product(sums, at, lines[k, inner], image[k])
+
+    def sum_over(sums, buf, n, me, peers):
+        part[...] = sums
+        buf[me] = sums
+        for to in peers:
             pltpu.make_async_remote_copy(
                 src_ref=part, dst_ref=buf.at[me], send_sem=s_sum.at[n], recv_sem=r_sum.at[n],
-                device_id=peer(to), device_id_type=MESH).start()
-            return 0
-
-        lax.fori_loop(1, 16, one, 0)
+                device_id=to, device_id_type=MESH).start()
         got = buf.at[pl.ds(0, 15)]
         pltpu.make_async_copy(got, got, r_sum.at[n]).wait()
         pltpu.make_async_copy(got, got, s_sum.at[n]).wait()
-        part[...] = jnp.sum(buf[...], axis=0)
-
-    sum_over(gather_a, 0, me_a, peer_a)
-    sum_over(gather_b, 1, me_b, peer_b)
-
-    totals = jnp.broadcast_to(jnp.sum(part[...], axis=1, keepdims=True), (16, COLS))
-    value = [totals[e : e + 1] for e in range(14)]
+        return jnp.sum(buf[...], axis=0)
+
+    def hops(d, n):
+        return min(d, n - d)
+
+    chip_x, core = spot // 2, spot % 2
+    steps = sorted(((x, y) for x in range(4) for y in range(4) if (x, y) != (0, 0)),
+                   key=lambda p: (-hops(p[0], 4) - hops(p[1], 4), p))
+    sums = sum_over(sums, gather_a, 0, chip_x * 4 + chip_y, [
+        ((gx // 8) * 8 + lax.rem(chip_x + x, 4) * 2 + core, lax.rem(chip_y + y, 4) * 2 + gy % 2)
+        for x, y in steps])
+    steps = sorted(((z, c) for z in range(8) for c in range(2) if (z, c) != (0, 0)),
+                   key=lambda p: (-hops(p[0], 8) - 0.5 * p[1], p))
+    peers = []
+    for z, c in steps:
+        to_z = lax.rem(chip_z + z, 8)
+        peers.append(((to_z // 2) * 8 + chip_x * 2 + (core + c) % 2, chip_y * 2 + to_z % 2))
+    sums = sum_over(sums, gather_b, 1, chip_z * 2 + core, peers)
+
+    value = [jnp.sum(jnp.where(lane == e, sums, 0.0), axis=1, keepdims=True) for e in range(14)]
     rhs = value[:BASIS]
     gram = {}
     at = BASIS
-    for k in range(BASIS - 1):
+    for k in range(BASIS):
         for m in range(k + 1):
             gram[m, k] = value[at]
             at += 1
-    for m in range(BASIS):
-        gram[m, BASIS - 1] = value[at]
-        at += 1
 
     low, pivot = {}, {}
     for j in range(BASIS):
@@ -597,14 +601,15 @@
         for m in range(i + 1, BASIS):
             sol[i] = sol[i] - low[m, i] * sol[m]
 
-    for k in range(BASIS):
-        wait_back(k)
+    for n in range(2):
+        wait_back(n)
     total = sol[0] * back[0]
     for k in range(1, BASIS):
         total = total + sol[k] * back[k]
     new_pot[...] = pot[...] + jnp.swapaxes(total, 0, 1)
 
     each_deep(wait_send)
+    each_halo(wait_send, fields.at[2], 1, s_pot, r_pot, False)
     wait_rows_sent(stage_cond, 0)
     wait_rows_sent(stage_res, 1)
     edges_sent(row_cond, cond_prev, cond_next, BASIS)
@@ -634,9 +639,9 @@
             pltpu.VMEM((EXT_Z, EXT_Y, COLS), f32),
             pltpu.VMEM((2, EXT_Z, EXT_Y, COLS), f32),
             pltpu.VMEM((EXT_Z, EXT_Y, COLS), f32),
+            pltpu.VMEM((EXT_Z, EXT_Y, COLS), f32),
             pltpu.VMEM((PLANES, ROWS, COLS), f32),
             pltpu.VMEM((WHOLE_Z, WHOLE_Z), f32),
-            pltpu.VMEM((ROWS, PLANES, COLS), f32),
             pltpu.VMEM((ROWS, PLANES, COLS), f32),
             pltpu.VMEM((ROWS, PLANES, COLS), f32),
             pltpu.VMEM(line, f32),
@@ -649,12 +654,12 @@
             pltpu.VMEM((BASIS, TILES, 8, COLS), f32),
             pltpu.VMEM(line, f32),
             pltpu.VMEM((BASIS, ROWS, PLANES, COLS), f32),
-            pltpu.VMEM((16, COLS), f32),
-            pltpu.VMEM((16, 16, COLS), f32),
-            pltpu.VMEM((16, 16, COLS), f32),
-            dma((8,)), dma((8,)), dma((8,)), dma((8,)), dma((8,)), dma((8,)),
+            pltpu.VMEM((1, COLS), f32),
+            pltpu.VMEM((16, 1, COLS), f32),
+            pltpu.VMEM((16, 1, COLS), f32),
+            dma((8,)), dma((8,)), dma((8,)), dma((8,)), dma((8,)), dma((8,)), dma((8,)), dma((8,)),
             dma((2,)), dma((2,)), dma((BASIS + 1, 2)), dma((BASIS + 1, 2)),
-            dma((BASIS,)), dma((BASIS,)), dma((2,)), dma((2,)), dma((2 + BASIS,)), dma((5,)),
+            dma((2,)), dma((2,)), dma((2,)), dma((2,)), dma((5,)), pltpu.SemaphoreType.REGULAR,
         ],
         compiler_params=pltpu.CompilerParams(
             collective_id=0, has_side_effects=True, vmem_limit_bytes=48 * 2**20),

time: 105 us -> 100 us (0.952)
  Pallas kernels: 98 us -> 93 us
    pallas_call x1, Pallas kernels: 98 us -> 93 us  [body(): pl.pallas_call(kernel, name='bidomain', out_shape=(block, block), in_spec...]
where the time goes in v2:
time: 100 us
  Pallas kernels  93 us (93%)
  local copies, waits for them, and re-layouts  6.55 us (7%)
    pallas_call x1, Pallas kernels, body(): pl.pallas_call(kernel, name='bidomain', out_shape=(block, block), in_spec...  93 us
    unnamed x14, local copies, waits for them, and re-layouts  6.55 us

profile of v2, /device:TPU:1, one launch (start us, length us, event | category | flops | bytes accessed | tf_op | source)
XLA Modules:
  0.0 100.2 jit_solution(12902517977509280331)
XLA Ops:
  0.6 0.0 copy-start
  0.6 0.9 copy-done
  1.6 0.0 copy-start.1
  1.6 0.9 copy-done.1
  2.5 0.0 copy-start.2
  2.5 0.9 copy-done.2
  3.4 0.0 copy-start.3
  3.4 0.9 copy-done.3
  4.3 0.0 copy-start.4
  4.3 0.9 copy-done.4
  5.2 0.0 copy-start.5
  5.2 0.7 copy-done.5
  5.9 93.0 %bidomain.1 = (f32[8,32,128]{2,1,0:T(8,128)S(1)}, f32[8,32,128]{2,1,0:T(8,128)S(1)}) custom-call(f32[2,9]{1,0:T(2,128)S(1)} %copy-done.5, f32[8,32,128]{2,1,0:T(8,128)S(1)} %copy-done.1, f32[8,32,128]{2,1,0:T(8,128)S(1)} %copy-done.2, s32[8,32,128]{2,1,0:T(8,128)S(1)} %copy-done.3, f32[8,32,128]{2,1,0:T(8,128)S(1)} %copy-done.4, f32[256,256]{1,0:T(8,128)S(1)} %copy-done), custom_call_target="tpu_custom_call" | custom-call | tf_op jit(solution)/shard_map/bidomain/pallas_call | solution.py:626
  98.9 0.7 copy.10
  99.5 0.7 copy.11
Async XLA Ops:
  0.6 1.0 copy-start
  1.6 0.9 copy-start.1
  2.5 0.9 copy-start.2
  3.4 0.9 copy-start.3
  4.3 0.9 copy-start.4
  5.2 0.7 copy-start.5

commit v3 on v2

--- a/solution.py
+++ b/solution.py
@@ -18,10 +18,15 @@
 PLANES, ROWS, COLS = 8, 32, 128
 HALO = 8
 EXT_Z, EXT_Y = PLANES + 2 * HALO, ROWS + 2 * HALO
+PAD_Y = EXT_Y + 16
+OWN = 8 + HALO
+EXT = pl.ds(8, EXT_Y)
 GX, GY = 32, 8
 WHOLE_Z = GX * PLANES
 WHOLE_Y = GY * ROWS
 TILES = WHOLE_Z // 8
+LINE = WHOLE_Z + 16
+LINES = pl.ds(8, WHOLE_Z)
 DIRECTIONS = tuple((a, b) for a in (-1, 0, 1) for b in (-1, 0, 1) if (a, b) != (0, 0))
 
 
@@ -35,32 +40,32 @@
 
 def y_range(b):
     if b == 0:
-        return pl.ds(HALO, ROWS), pl.ds(HALO, ROWS)
+        return pl.ds(OWN, ROWS), pl.ds(OWN, ROWS)
     if b > 0:
-        return pl.ds(HALO + ROWS - 8, 8), pl.ds(0, 8)
-    return pl.ds(HALO, 8), pl.ds(HALO + ROWS, 8)
-
-
-def lane_shifts(v, first, last):
-    up = jnp.where(last, 0.0, pltpu.roll(v, COLS - 1, 1))
-    down = jnp.where(first, 0.0, pltpu.roll(v, 1, 1))
-    return up, down
-
-
-def stencil(minus, here, plus, k, first, last, swapped=False):
-    rows = here.shape[0]
-    lead, sub, lane = (k[1], k[0], k[2]) if swapped else (k[0], k[1], k[2])
-    both, cross = k[3], k[4]
-    lead_lane, lead_lane_cross = (k[7], k[8]) if swapped else (k[5], k[6])
-    sub_lane, sub_lane_cross = (k[5], k[6]) if swapped else (k[7], k[8])
-    right, left = lane_shifts(here, first, last)
-    up = sub * here + both * plus + cross * minus + sub_lane * right + sub_lane_cross * left
-    down = sub * here + both * minus + cross * plus + sub_lane * left + sub_lane_cross * right
-    x_up = lane * here + lead_lane * plus + lead_lane_cross * minus
-    x_down = lane * here + lead_lane * minus + lead_lane_cross * plus
-    x_up = jnp.where(last, 0.0, pltpu.roll(x_up, COLS - 1, 1))
-    x_down = jnp.where(first, 0.0, pltpu.roll(x_down, 1, 1))
-    return lead * (plus + minus) + pltpu.roll(up, rows - 1, 0) + pltpu.roll(down, 1, 0) + x_up + x_down
+        return pl.ds(OWN + ROWS - 8, 8), pl.ds(OWN - 8, 8)
+    return pl.ds(OWN, 8), pl.ds(OWN + ROWS, 8)
+
+
+def combine(k, lead, sub, lane, lead_sub, lead_lane, sub_lane, scale=1.0):
+    half = 0.5 * scale
+    return dict(
+        lead=scale * k[lead], sub=scale * k[sub], lane=scale * k[lane],
+        both=scale * k[lead_sub], cross=scale * k[lead_sub + 1],
+        lead_sum=half * (k[lead_lane] + k[lead_lane + 1]), lead_diff=half * (k[lead_lane] - k[lead_lane + 1]),
+        sub_sum=half * (k[sub_lane] + k[sub_lane + 1]), sub_diff=half * (k[sub_lane] - k[sub_lane + 1]))
+
+
+def stencil(read, k, first, last):
+    here, plus, minus = read(0, 0), read(1, 0), read(-1, 0)
+    up, down = read(0, 1), read(0, -1)
+    total, diff = plus + minus, plus - minus
+    rows, row_diff = up + down, up - down
+    even = k["lane"] * here + k["lead_sum"] * total + k["sub_sum"] * rows
+    odd = k["lead_diff"] * diff + k["sub_diff"] * row_diff
+    out = k["lead"] * total + k["sub"] * rows
+    out = out + k["both"] * (read(1, 1) + read(-1, -1)) + k["cross"] * (read(1, -1) + read(-1, 1))
+    out = out + jnp.where(last, 0.0, pltpu.roll(even + odd, COLS - 1, 1))
+    return out + jnp.where(first, 0.0, pltpu.roll(even - odd, 1, 1))
 
 
 def owner(row):
@@ -85,10 +90,10 @@
 def kernel(
     coup, volt_in, pot_in, tissue_in, gain_in, factor_in, new_volt, new_pot,
     volt, pot, tissue, gain, factor,
-    fields, resid, upd, diag, estimate, own_term, matrix,
+    fields, resid, upd, diag, estimate, weighted, own_term, matrix,
     stage_cond, stage_res,
     row_cond, row_res, lines, line_prev, line_next, cond_prev, cond_next,
-    image, row_diag, back, part, gather_a, gather_b,
+    line_weighted, image, row_diag, back, part, gather_a, gather_b,
     s_fields, r_fields, s_cond, r_cond, s_pot, r_pot, s_resid, r_resid,
     s_rows, r_rows, s_edge, r_edge, s_back, r_back, s_sum, r_sum, s_take, far,
 ):
@@ -107,6 +112,13 @@
     def at_y(y):
         return gx, y * 2 + gy % 2
 
+    takes = [
+        pltpu.make_async_copy(src, dst, s_take.at[n])
+        for n, (src, dst) in enumerate(
+            ((tissue_in, tissue), (gain_in, gain), (volt_in, volt), (pot_in, pot), (factor_in, factor)))
+    ]
+    for copy in takes:
+        copy.start()
     barrier = pltpu.get_barrier_semaphore()
 
     def greet(sem, to):
@@ -119,13 +131,6 @@
         greet(barrier, ((gx // 8) * 8 + lax.rem(spot + d, 8), gy))
     for d in range(1, 4):
         greet(barrier, at_y(lax.rem(chip_y + d, 4)))
-    takes = [
-        pltpu.make_async_copy(src, dst, s_take.at[n])
-        for n, (src, dst) in enumerate(
-            ((tissue_in, tissue), (gain_in, gain), (volt_in, volt), (pot_in, pot), (factor_in, factor)))
-    ]
-    for copy in takes:
-        copy.start()
     for copy in takes:
         copy.wait()
 
@@ -133,6 +138,10 @@
     first, last = lane == 0, lane == COLS - 1
     k_in = [coup[0, n] for n in range(9)]
     k_ex = [coup[1, n] for n in range(9)]
+    z_twice = combine(k_in, 0, 1, 2, 3, 5, 7, time_step)
+    z_extra = combine(k_ex, 0, 1, 2, 3, 5, 7)
+    line_in = combine(k_in, 1, 0, 2, 3, 7, 5)
+    line_ex = combine(k_ex, 1, 0, 2, 3, 7, 5)
 
     def neighbour(a, b):
         ok = (gx + a >= 0) & (gx + a < GX) & (gy + b >= 0) & (gy + b < GY)
@@ -189,33 +198,39 @@
 
     own_group = own_gy == gy
 
+    def row_tile(i):
+        return pl.ds(pl.multiple_of(8 + 8 * i, 8), 8)
+
+    turned = chip_y % 2
+    upper = gy % 2 + turned * (1 - 2 * (gy % 2))
+
     def scatter_rows(stage, rows_ref, n):
-        def one(t, _):
-            to_gx, to_gy = owner(gy * ROWS + t)
-
-            @pl.when((to_gx != gx) | (to_gy != gy))
-            def _():
-                pltpu.make_async_remote_copy(
-                    src_ref=stage.at[t], dst_ref=rows_ref.at[1 + gx],
-                    send_sem=s_rows.at[n], recv_sem=r_rows.at[n],
-                    device_id=(to_gx, to_gy), device_id_type=MESH).start()
-            return 0
-
-        lax.fori_loop(0, ROWS, one, 0, unroll=4)
+        for z in range(4):
+            for q in range(8):
+                m = z * 8 + (q if z % 2 == 0 else 7 - q)
+                t = m + turned * (31 - 2 * m)
+                to_gx, to_gy = upper * 16 + (z // 2) * 8 + q, chip_y * 2 + z % 2
+
+                @pl.when((to_gx != gx) | (to_gy != gy))
+                def _():
+                    pltpu.make_async_remote_copy(
+                        src_ref=stage.at[t], dst_ref=rows_ref.at[row_tile(gx)],
+                        send_sem=s_rows.at[n], recv_sem=r_rows.at[n],
+                        device_id=(to_gx, to_gy), device_id_type=MESH).start()
 
         @pl.when(own_group)
         def _():
-            rows_ref[1 + gx] = stage[own_t]
+            rows_ref[row_tile(gx)] = stage[own_t]
 
     def wait_rows(stage, rows_ref, n):
         @pl.when(own_group)
         def _():
-            part_ref = rows_ref.at[pl.ds(1, TILES - 1)]
+            part_ref = rows_ref.at[pl.ds(8, WHOLE_Z - 8)]
             pltpu.make_async_copy(part_ref, part_ref, r_rows.at[n]).wait()
 
         @pl.when(jnp.logical_not(own_group))
         def _():
-            part_ref = rows_ref.at[pl.ds(1, TILES)]
+            part_ref = rows_ref.at[LINES]
             pltpu.make_async_copy(part_ref, part_ref, r_rows.at[n]).wait()
 
     def wait_rows_sent(stage, n):
@@ -228,15 +243,13 @@
         def _():
             pltpu.make_async_copy(stage, stage, s_rows.at[n]).wait()
 
-    def send_back(n):
-        two = pl.ds(2 * n, 2)
-
+    def send_back(k):
         def one(i, _):
             @pl.when((i != gx) | (own_gy != gy))
             def _():
                 pltpu.make_async_remote_copy(
-                    src_ref=lines.at[two, 1 + i], dst_ref=back.at[two, own_t],
-                    send_sem=s_back.at[n], recv_sem=r_back.at[n],
+                    src_ref=lines.at[k, row_tile(i)], dst_ref=back.at[k, own_t],
+                    send_sem=s_back.at[k], recv_sem=r_back.at[k],
                     device_id=(i, own_gy), device_id_type=MESH).start()
             return 0
 
@@ -244,25 +257,21 @@
 
         @pl.when(own_group)
         def _():
-            for k in (2 * n, 2 * n + 1):
-                back[k, own_t] = lines[k, 1 + gx]
-
-    def wait_back(n):
-        two = pl.ds(2 * n, 2)
-
+            back[k, own_t] = lines[k, row_tile(gx)]
+
+    def wait_back(k):
         @pl.when(own_group)
         def _():
-            got = back.at[two, pl.ds(0, ROWS - 1)]
-            pltpu.make_async_copy(got, got, r_back.at[n]).wait()
-            pltpu.make_async_copy(got, got, s_back.at[n]).wait()
+            got = back.at[k, pl.ds(0, ROWS - 1)]
+            pltpu.make_async_copy(got, got, r_back.at[k]).wait()
+            pltpu.make_async_copy(got, got, s_back.at[k]).wait()
 
         @pl.when(jnp.logical_not(own_group))
         def _():
-            got = back.at[two]
-            pltpu.make_async_copy(got, got, r_back.at[n]).wait()
-            pltpu.make_async_copy(got, got, s_back.at[n]).wait()
-
-    inner = pl.ds(1, TILES)
+            pltpu.make_async_copy(back.at[k], back.at[k], r_back.at[k]).wait()
+            pltpu.make_async_copy(back.at[k], back.at[k], s_back.at[k]).wait()
+
+    inner = LINES
 
     def edge(src, dst, n, side):
         to_gx, to_gy = owner(row + (1 if side == 0 else -1))
@@ -300,7 +309,7 @@
         def _():
             edge(src, nxt, n, 1).wait_send()
 
-    own_y = pl.ds(HALO, ROWS)
+    own_y = pl.ds(OWN, ROWS)
     conduct = tissue[...].astype(jnp.float32) * gain[...]
     own = (pl.ds(HALO, PLANES), own_y, slice(None))
     fields[0, *own] = volt[...] + pot[...]
@@ -309,8 +318,8 @@
     pl.semaphore_wait(barrier, 25)
     near = fields.at[pl.ds(0, 2)]
     each_halo(start, near, 1, s_fields, r_fields, True)
+    each_halo(start, fields.at[2], 1, s_pot, r_pot, False)
     each_deep(start)
-    each_halo(start, fields.at[2], 1, s_pot, r_pot, False)
     for d in range(1, 8):
         greet(far, at_z(lax.rem(chip_z + d, 8)))
     for d in range(1, 4):
@@ -332,26 +341,36 @@
             resid[zd, yd, :] = jnp.zeros(shape, jnp.float32)
     stage_cond[...] = jnp.swapaxes(conduct, 0, 1)
     tile = jnp.zeros((8, COLS), jnp.float32)
-    for ref in (row_cond, row_res, cond_prev, cond_next):
-        ref[0] = tile
-        ref[TILES + 1] = tile
-    for k in range(BASIS):
-        for ref in (lines, line_prev, line_next):
-            ref[k, 0] = tile
-            ref[k, TILES + 1] = tile
-    blank = jnp.zeros((TILES, 8, COLS), jnp.float32)
+    beyond = (pl.ds(0, 8), pl.ds(PAD_Y - 8, 8))
+
+    def blank_rows(z, _):
+        for rows in beyond:
+            fields[1, z, rows, :] = tile
+            weighted[0, z, rows, :] = tile
+            weighted[1, z, rows, :] = tile
+        return 0
+
+    lax.fori_loop(0, EXT_Z, blank_rows, 0)
+    ends = (pl.ds(0, 8), pl.ds(LINE - 8, 8))
+    for rows in ends:
+        for ref in (row_cond, row_res, cond_prev, cond_next):
+            ref[rows] = tile
+        for k in range(BASIS):
+            for ref in (lines, line_prev, line_next):
+                ref[k, rows] = tile
+    blank = jnp.zeros((WHOLE_Z, COLS), jnp.float32)
 
     @pl.when(jnp.logical_not(has_prev))
     def _():
-        cond_prev[pl.ds(1, TILES)] = blank
+        cond_prev[LINES] = blank
         for k in range(BASIS):
-            line_prev[k, pl.ds(1, TILES)] = blank
+            line_prev[k, LINES] = blank
 
     @pl.when(jnp.logical_not(has_next))
     def _():
-        cond_next[pl.ds(1, TILES)] = blank
+        cond_next[LINES] = blank
         for k in range(BASIS):
-            line_next[k, pl.ds(1, TILES)] = blank
+            line_next[k, LINES] = blank
 
     whole = lax.dot_general(
         factor[...], factor[...], (((0,), (0,)), ((), ())), precision=HIGHEST,
@@ -378,70 +397,78 @@
 
     each_halo(wait_recv, near, 1, s_fields, r_fields, True, receive=True)
 
+    def moved(ref, z, at, rows):
+        return lambda i, j: ref[z + i, pl.ds(at + j, rows), :]
+
+    cond = fields.at[1]
+
+    def weigh(z, _):
+        weighted[0, z, EXT, :] = cond[z, EXT, :] * (fields[0, z, EXT, :])
+        return 0
+
+    lax.fori_loop(HALO - 1, HALO + PLANES + 1, weigh, 0)
+
     def first_plane(z, _):
-        s = stencil(fields[1, z - 1], fields[1, z], fields[1, z + 1], k_in, first, last)
-        diag[z] = s
-        w = [fields[1, z + n] * fields[0, z + n] for n in (-1, 0, 1)]
-        ki = fields[1, z] * (s * fields[0, z] - stencil(*w, k_in, first, last))
-        resid[z, own_y, :] = own_term[z - HALO] - time_step * ki[HALO : HALO + ROWS]
+        s = stencil(moved(cond, z, OWN, ROWS), z_twice, first, last)
+        flux = s * fields[0, z, own_y, :] - stencil(moved(weighted.at[0], z, OWN, ROWS), z_twice, first, last)
+        resid[z, own_y, :] = own_term[z - HALO] - cond[z, own_y, :] * flux
         return 0
 
     lax.fori_loop(HALO, HALO + PLANES, first_plane, 0)
     each_halo(start, resid, HALO, s_resid, r_resid, False)
 
-    each_deep(wait_recv, receive=True)
-
-    def diag_plane(z, _):
-        diag[z] = stencil(fields[1, z - 1], fields[1, z], fields[1, z + 1], k_in, first, last)
-        return 0
-
-    lax.fori_loop(1, HALO, diag_plane, 0)
-    lax.fori_loop(HALO + PLANES, EXT_Z - 1, diag_plane, 0)
     each_halo(wait_recv, fields.at[2], 1, s_pot, r_pot, False, receive=True)
     ex_total = 2.0 * ex_sum
 
     def extra_plane(z, _):
-        p = [fields[2, z + m] for m in (-1, 0, 1)]
-        ke = stencil(*p, k_ex, first, last) - ex_total * p[1]
-        own_term[z - HALO] = ke[HALO : HALO + ROWS]
+        ke = stencil(moved(fields.at[2], z, OWN, ROWS), z_extra, first, last)
+        own_term[z - HALO] = ke - ex_total * fields[2, z, own_y, :]
         return 0
 
     lax.fori_loop(HALO, HALO + PLANES, extra_plane, 0)
+    each_deep(wait_recv, receive=True)
+
+    def diag_plane(z, _):
+        diag[z, EXT, :] = 1.0 + cond[z, EXT, :] * stencil(moved(cond, z, 8, EXT_Y), z_twice, first, last)
+        return 0
+
+    lax.fori_loop(1, EXT_Z - 1, diag_plane, 0)
     each_halo(wait_send, near, 1, s_fields, r_fields, True)
     pl.semaphore_wait(far, 10)
+    scatter_rows(stage_cond, row_cond, 0)
     each_halo(wait_recv, resid, HALO, s_resid, r_resid, False, receive=True)
 
-    scatter_rows(stage_cond, row_cond, 0)
-
     inv_centre = 1.0 / centre
 
     def first_update(z, _):
-        u = resid[z] * inv_centre
-        upd[0, z] = u
-        estimate[z] = u
+        u = resid[z, EXT, :] * inv_centre
+        upd[z, EXT, :] = u
+        estimate[z, EXT, :] = u
+        weighted[0, z, EXT, :] = cond[z, EXT, :] * u
         return 0
 
     lax.fori_loop(0, EXT_Z, first_update, 0)
 
     def sweep(n, weight):
-        old = lax.rem(n + 1, 2)
+        old = weighted.at[lax.rem(n + 1, 2)]
         new = lax.rem(n, 2)
         weight_next = 1.0 / (2.0 * ratio - weight)
         keep = weight_next * weight
         gain_r = 2.0 * weight_next / half
 
+        def one(z):
+            u = upd[z, EXT, :]
+            c = cond[z, EXT, :]
+            r = resid[z, EXT, :] - diag[z, EXT, :] * u + c * stencil(moved(old, z, 8, EXT_Y), z_twice, first, last)
+            resid[z, EXT, :] = r
+            fresh = keep * u + gain_r * r
+            upd[z, EXT, :] = fresh
+            estimate[z, EXT, :] = estimate[z, EXT, :] + fresh
+            weighted[new, z, EXT, :] = c * fresh
+
         def pair(i, _):
-            z = n + 2 * i
-            c = [fields[1, z + m] for m in (-1, 0, 1, 2)]
-            u = [upd[old, z + m] for m in (-1, 0, 1, 2)]
-            w = [a * b for a, b in zip(c, u)]
-            for m in (1, 2):
-                ki = c[m] * (diag[z + m - 1] * u[m] - stencil(*w[m - 1 : m + 2], k_in, first, last))
-                r = resid[z + m - 1] - (u[m] + time_step * ki)
-                resid[z + m - 1] = r
-                fresh = keep * u[m] + gain_r * r
-                upd[new, z + m - 1] = fresh
-                estimate[z + m - 1] = estimate[z + m - 1] + fresh
+            one(n + 2 * i)
+            one(n + 2 * i + 1)
             return 0
 
         lax.fori_loop(0, EXT_Z // 2 - n, pair, 0)
@@ -454,15 +481,17 @@
     lax.fori_loop(CHEB - 2, CHEB, sweep, weight)
 
     def total_plane(z, _):
-        fields[0, z] = fields[0, z] + estimate[z]
+        total = fields[0, z, EXT, :] + estimate[z, EXT, :]
+        fields[0, z, EXT, :] = total
+        weighted[0, z, EXT, :] = cond[z, EXT, :] * total
         return 0
 
     lax.fori_loop(HALO - 1, HALO + PLANES + 1, total_plane, 0)
 
     def elliptic_plane(z, _):
-        w = [fields[1, z + m] * fields[0, z + m] for m in (-1, 0, 1)]
-        ki = fields[1, z] * (diag[z] * fields[0, z] - stencil(*w, k_in, first, last))
-        own_term[z - HALO] = own_term[z - HALO] - ki[HALO : HALO + ROWS]
+        twice = (diag[z, own_y, :] - 1.0) * fields[0, z, own_y, :]
+        twice = twice - cond[z, own_y, :] * stencil(moved(weighted.at[0], z, OWN, ROWS), z_twice, first, last)
+        own_term[z - HALO] = own_term[z - HALO] - twice / time_step
         return 0
 
     lax.fori_loop(HALO, HALO + PLANES, elliptic_plane, 0)
@@ -473,12 +502,10 @@
     wait_rows(stage_res, row_res, 1)
 
     def apply_matrix(src, k, shift=None):
-        out = jnp.dot(matrix[...], src.reshape(WHOLE_Z, COLS), precision=HIGHEST,
-                      preferred_element_type=jnp.float32)
-        out = out.reshape(TILES, 8, COLS)
+        out = jnp.dot(matrix[...], src, precision=HIGHEST, preferred_element_type=jnp.float32)
         if shift is not None:
-            out = out - shift * lines[k - 1, inner]
-        lines[k, inner] = out
+            out = out - shift * lines[k - 1, LINES]
+        lines[k, LINES] = out
 
     sums = jnp.zeros((1, COLS), jnp.float32)
 
@@ -487,40 +514,35 @@
         total = jnp.sum(jnp.sum(total, axis=0), axis=0, keepdims=True)
         return sums + jnp.where(lane == e, jnp.sum(total, axis=1, keepdims=True), 0.0)
 
-    CHUNK = 8
-
-    def chunk(ref, at):
-        return ref[pl.ds(at, CHUNK + 2)].reshape((CHUNK + 2) * 8, COLS)
-
-    def put(ref, at, value):
-        ref[pl.ds(at, CHUNK)] = value[8 : 8 + CHUNK * 8].reshape(CHUNK, 8, COLS)
+    CHUNK = 64
+
+    def near_rows(refs, at):
+        return lambda i, j: refs[i + 1][pl.ds(at + j, CHUNK), :]
+
+    weigh_refs = [line_weighted.at[n] for n in range(3)]
+    cond_refs = [cond_prev, row_cond, cond_next]
 
     def operate(k):
-        def one(i, _):
-            at = i * CHUNK
-            c = [chunk(r, at) for r in (cond_prev, row_cond, cond_next)]
-            s = [chunk(r, at) for r in (line_prev.at[k], lines.at[k], line_next.at[k])]
-            w = [a * b for a, b in zip(c, s)]
-            ki = c[1] * (chunk(row_diag, at) * s[1] - stencil(*w, k_in, first, last, True))
-            ke = ex_total * s[1] - stencil(*s, k_ex, first, last, True)
-            put(image.at[k], at, ki + ke)
-            return 0
-
-        lax.fori_loop(0, TILES // CHUNK, one, 0)
-
-    def line_diag(i, _):
-        at = i * CHUNK
-        c = [chunk(r, at) for r in (cond_prev, row_cond, cond_next)]
-        row_diag[pl.ds(at + 1, CHUNK)] = stencil(*c, k_in, first, last, True)[8 : 8 + CHUNK * 8].reshape(
-            CHUNK, 8, COLS)
-        return 0
+        basis = [line_prev.at[k], lines.at[k], line_next.at[k]]
+        for n in (0, 2):
+            weigh_refs[n][...] = cond_refs[n][...] * basis[n][...]
+        for at in range(8, 8 + WHOLE_Z, CHUNK):
+            rows = pl.ds(at, CHUNK)
+            s = lines[k, rows]
+            ki = row_diag[rows] * s - row_cond[rows] * stencil(near_rows(weigh_refs, at), line_in, first, last)
+            image[k, pl.ds(at - 8, CHUNK)] = ki - stencil(near_rows(basis, at), line_ex, first, last)
+
+    def line_diag():
+        for at in range(8, 8 + WHOLE_Z, CHUNK):
+            rows = pl.ds(at, CHUNK)
+            row_diag[rows] = ex_total + row_cond[rows] * stencil(near_rows(cond_refs, at), line_in, first, last)
 
     apply_matrix(row_res[inner], 0)
     edges_start(lines.at[0], line_prev.at[0], line_next.at[0], 0)
+    send_back(0)
+    weigh_refs[1][...] = row_cond[...] * lines[0]
     edges_wait(row_cond, cond_prev, cond_next, BASIS)
-    row_diag[0] = tile
-    row_diag[TILES + 1] = tile
-    lax.fori_loop(0, TILES // CHUNK, line_diag, 0)
+    line_diag()
     sums = product(sums, 0, lines[0, inner], row_res[inner])
 
     at = BASIS
@@ -530,8 +552,8 @@
         if k < BASIS - 1:
             apply_matrix(image[k], k + 1, shift)
             edges_start(lines.at[k + 1], line_prev.at[k + 1], line_next.at[k + 1], k + 1)
-            if k % 2 == 0:
-                send_back(k // 2)
+            send_back(k + 1)
+            weigh_refs[1][...] = row_cond[...] * lines[k + 1]
             sums = product(sums, k + 1, lines[k + 1, inner], row_res[inner])
             for m in range(k + 1):
                 sums = product(sums, at, lines[m, inner], image[k])
@@ -601,8 +623,8 @@
         for m in range(i + 1, BASIS):
             sol[i] = sol[i] - low[m, i] * sol[m]
 
-    for n in range(2):
-        wait_back(n)
+    for k in range(BASIS):
+        wait_back(k)
     total = sol[0] * back[0]
     for k in range(1, BASIS):
         total = total + sol[k] * back[k]
@@ -621,7 +643,7 @@
     f32 = jnp.float32
     block = jax.ShapeDtypeStruct((PLANES, ROWS, COLS), f32)
     vmem = pl.BlockSpec(memory_space=pltpu.VMEM)
-    line = (TILES + 2, 8, COLS)
+    line = (LINE, COLS)
     dma = pltpu.SemaphoreType.DMA
     return pl.pallas_call(
         kernel,
@@ -635,11 +657,12 @@
             pltpu.VMEM((PLANES, ROWS, COLS), jnp.int32),
             pltpu.VMEM((PLANES, ROWS, COLS), f32),
             pltpu.VMEM((WHOLE_Z, WHOLE_Z), f32),
-            pltpu.VMEM((3, EXT_Z, EXT_Y, COLS), f32),
-            pltpu.VMEM((EXT_Z, EXT_Y, COLS), f32),
-            pltpu.VMEM((2, EXT_Z, EXT_Y, COLS), f32),
-            pltpu.VMEM((EXT_Z, EXT_Y, COLS), f32),
-            pltpu.VMEM((EXT_Z, EXT_Y, COLS), f32),
+            pltpu.VMEM((3, EXT_Z, PAD_Y, COLS), f32),
+            pltpu.VMEM((EXT_Z, PAD_Y, COLS), f32),
+            pltpu.VMEM((EXT_Z, PAD_Y, COLS), f32),
+            pltpu.VMEM((EXT_Z, PAD_Y, COLS), f32),
+            pltpu.VMEM((EXT_Z, PAD_Y, COLS), f32),
+            pltpu.VMEM((2, EXT_Z, PAD_Y, COLS), f32),
             pltpu.VMEM((PLANES, ROWS, COLS), f32),
             pltpu.VMEM((WHOLE_Z, WHOLE_Z), f32),
             pltpu.VMEM((ROWS, PLANES, COLS), f32),
@@ -651,7 +674,8 @@
             pltpu.VMEM((BASIS, *line), f32),
             pltpu.VMEM(line, f32),
             pltpu.VMEM(line, f32),
-            pltpu.VMEM((BASIS, TILES, 8, COLS), f32),
+            pltpu.VMEM((3, *line), f32),
+            pltpu.VMEM((BASIS, WHOLE_Z, COLS), f32),
             pltpu.VMEM(line, f32),
             pltpu.VMEM((BASIS, ROWS, PLANES, COLS), f32),
             pltpu.VMEM((1, COLS), f32),
@@ -659,7 +683,7 @@
             pltpu.VMEM((16, 1, COLS), f32),
             dma((8,)), dma((8,)), dma((8,)), dma((8,)), dma((8,)), dma((8,)), dma((8,)), dma((8,)),
             dma((2,)), dma((2,)), dma((BASIS + 1, 2)), dma((BASIS + 1, 2)),
-            dma((2,)), dma((2,)), dma((2,)), dma((2,)), dma((5,)), pltpu.SemaphoreType.REGULAR,
+            dma((BASIS,)), dma((BASIS,)), dma((2,)), dma((2,)), dma((5,)), pltpu.SemaphoreType.REGULAR,
         ],
         compiler_params=pltpu.CompilerParams(
             collective_id=0, has_side_effects=True, vmem_limit_bytes=48 * 2**20),

time: 100 us -> 98.7 us (0.987)
  Pallas kernels: 93 us -> 91.3 us
    pallas_call x1, Pallas kernels: 93 us -> 91.3 us  [body(): pl.pallas_call(kernel, name='bidomain', out_shape=(block, block), in_spec...]
where the time goes in v3:
time: 98.7 us; the launch traced here: 98.5 us
  Pallas kernels  91.3 us (93%)
  local copies, waits for them, and re-layouts  6.55 us (7%)
    pallas_call x1, Pallas kernels, body(): pl.pallas_call(kernel, name='bidomain', out_shape=(block, block), in_spec...  91.3 us
    unnamed x14, local copies, waits for them, and re-layouts  6.55 us

profile of v3, /device:TPU:1, one launch (start us, length us, event | category | flops | bytes accessed | tf_op | source)
XLA Modules:
  0.0 98.5 jit_solution(11730215518551770731)
XLA Ops:
  0.6 0.0 copy-start
  0.6 0.9 copy-done
  1.6 0.0 copy-start.1
  1.6 0.9 copy-done.1
  2.5 0.0 copy-start.2
  2.5 0.9 copy-done.2
  3.4 0.0 copy-start.3
  3.4 0.9 copy-done.3
  4.3 0.0 copy-start.4
  4.3 0.9 copy-done.4
  5.2 0.0 copy-start.5
  5.2 0.7 copy-done.5
  5.9 91.3 %bidomain.1 = (f32[8,32,128]{2,1,0:T(8,128)S(1)}, f32[8,32,128]{2,1,0:T(8,128)S(1)}) custom-call(f32[2,9]{1,0:T(2,128)S(1)} %copy-done.5, f32[8,32,128]{2,1,0:T(8,128)S(1)} %copy-done.1, f32[8,32,128]{2,1,0:T(8,128)S(1)} %copy-done.2, s32[8,32,128]{2,1,0:T(8,128)S(1)} %copy-done.3, f32[8,32,128]{2,1,0:T(8,128)S(1)} %copy-done.4, f32[256,256]{1,0:T(8,128)S(1)} %copy-done), custom_call_target="tpu_custom_call" | custom-call | tf_op jit(solution)/shard_map/bidomain/pallas_call | solution.py:648
  97.2 0.7 copy.10
  97.9 0.7 copy.11
Async XLA Ops:
  0.6 1.0 copy-start
  1.6 0.9 copy-start.1
  2.5 0.9 copy-start.2
  3.4 0.9 copy-start.3
  4.3 0.9 copy-start.4
  5.2 0.7 copy-start.5

commit v4 on v3

--- a/solution.py
+++ b/solution.py
@@ -55,6 +55,26 @@
         sub_sum=half * (k[sub_lane] + k[sub_lane + 1]), sub_diff=half * (k[sub_lane] - k[sub_lane + 1]))
 
 
+def shift_lanes(even, odd, first, last):
+    right = jnp.where(last, 0.0, pltpu.roll(even + odd, COLS - 1, 1))
+    return right + jnp.where(first, 0.0, pltpu.roll(even - odd, 1, 1))
+
+
+def stencil_here(read, k, first, last):
+    up, down = read(0, 1), read(0, -1)
+    rows = up + down
+    even = k["lane"] * read(0, 0) + k["sub_sum"] * rows
+    return k["sub"] * rows + shift_lanes(even, k["sub_diff"] * (up - down), first, last)
+
+
+def stencil_beside(read, k, first, last):
+    plus, minus = read(1, 0), read(-1, 0)
+    total = plus + minus
+    out = k["lead"] * total
+    out = out + k["both"] * (read(1, 1) + read(-1, -1)) + k["cross"] * (read(1, -1) + read(-1, 1))
+    return out + shift_lanes(k["lead_sum"] * total, k["lead_diff"] * (plus - minus), first, last)
+
+
 def stencil(read, k, first, last):
     here, plus, minus = read(0, 0), read(1, 0), read(-1, 0)
     up, down = read(0, 1), read(0, -1)
@@ -64,8 +84,7 @@
     odd = k["lead_diff"] * diff + k["sub_diff"] * row_diff
     out = k["lead"] * total + k["sub"] * rows
     out = out + k["both"] * (read(1, 1) + read(-1, -1)) + k["cross"] * (read(1, -1) + read(-1, 1))
-    out = out + jnp.where(last, 0.0, pltpu.roll(even + odd, COLS - 1, 1))
-    return out + jnp.where(first, 0.0, pltpu.roll(even - odd, 1, 1))
+    return out + shift_lanes(even, odd, first, last)
 
 
 def owner(row):
@@ -382,7 +401,10 @@
         ex_sum = ex_sum + k_ex[n]
     reach = jnp.max(jnp.sum(jnp.abs(whole), axis=1, keepdims=True), axis=0, keepdims=True)
     bound = reach * (4.0 * gain_top * in_sum + 4.0 * ex_sum)
-    matrix[...] = whole * (1.0 / bound)
+    scaled = whole * (1.0 / bound)
+    coarse = scaled.astype(jnp.bfloat16)
+    matrix[0] = coarse
+    matrix[1] = (scaled - coarse.astype(jnp.float32)).astype(jnp.bfloat16)
     eye = lax.broadcasted_iota(jnp.int32, whole.shape, 0) == lax.broadcasted_iota(jnp.int32, whole.shape, 1)
     mean = jnp.sum(jnp.sum(jnp.where(eye, whole, 0.0), axis=1, keepdims=True), axis=0, keepdims=True) / WHOLE_Z
     shift = SHIFT * mean * (2.0 * in_sum + 2.0 * ex_sum) / bound
@@ -460,15 +482,16 @@
             u = upd[z, EXT, :]
             c = cond[z, EXT, :]
             r = resid[z, EXT, :] - diag[z, EXT, :] * u + c * stencil(moved(old, z, 8, EXT_Y), z_twice, first, last)
-            resid[z, EXT, :] = r
             fresh = keep * u + gain_r * r
-            upd[z, EXT, :] = fresh
-            estimate[z, EXT, :] = estimate[z, EXT, :] + fresh
-            weighted[new, z, EXT, :] = c * fresh
+            return r, fresh, estimate[z, EXT, :] + fresh, c * fresh
 
         def pair(i, _):
-            one(n + 2 * i)
-            one(n + 2 * i + 1)
+            planes = [n + 2 * i, n + 2 * i + 1]
+            for z, (r, fresh, total, flux) in zip(planes, [one(z) for z in planes]):
+                resid[z, EXT, :] = r
+                upd[z, EXT, :] = fresh
+                estimate[z, EXT, :] = total
+                weighted[new, z, EXT, :] = flux
             return 0
 
         lax.fori_loop(0, EXT_Z // 2 - n, pair, 0)
@@ -502,7 +525,13 @@
     wait_rows(stage_res, row_res, 1)
 
     def apply_matrix(src, k, shift=None):
-        out = jnp.dot(matrix[...], src, precision=HIGHEST, preferred_element_type=jnp.float32)
+        coarse = src.astype(jnp.bfloat16)
+        fine = (src - coarse.astype(jnp.float32)).astype(jnp.bfloat16)
+
+        def dot(a, b):
+            return jnp.dot(a, b, preferred_element_type=jnp.float32)
+
+        out = dot(matrix[0], fine) + dot(matrix[1], coarse) + dot(matrix[0], coarse)
         if shift is not None:
             out = out - shift * lines[k - 1, LINES]
         lines[k, LINES] = out
@@ -522,15 +551,23 @@
     weigh_refs = [line_weighted.at[n] for n in range(3)]
     cond_refs = [cond_prev, row_cond, cond_next]
 
-    def operate(k):
-        basis = [line_prev.at[k], lines.at[k], line_next.at[k]]
+    def operate_here(k):
+        basis = [None, lines.at[k], None]
+        for at in range(8, 8 + WHOLE_Z, CHUNK):
+            rows = pl.ds(at, CHUNK)
+            ki = row_diag[rows] * lines[k, rows]
+            ki = ki - row_cond[rows] * stencil_here(near_rows(weigh_refs, at), line_in, first, last)
+            image[k, pl.ds(at - 8, CHUNK)] = ki - stencil_here(near_rows(basis, at), line_ex, first, last)
+
+    def operate_beside(k):
+        basis = [line_prev.at[k], None, line_next.at[k]]
         for n in (0, 2):
             weigh_refs[n][...] = cond_refs[n][...] * basis[n][...]
         for at in range(8, 8 + WHOLE_Z, CHUNK):
             rows = pl.ds(at, CHUNK)
-            s = lines[k, rows]
-            ki = row_diag[rows] * s - row_cond[rows] * stencil(near_rows(weigh_refs, at), line_in, first, last)
-            image[k, pl.ds(at - 8, CHUNK)] = ki - stencil(near_rows(basis, at), line_ex, first, last)
+            ki = row_cond[rows] * stencil_beside(near_rows(weigh_refs, at), line_in, first, last)
+            ki = ki + stencil_beside(near_rows(basis, at), line_ex, first, last)
+            image[k, pl.ds(at - 8, CHUNK)] = image[k, pl.ds(at - 8, CHUNK)] - ki
 
     def line_diag():
         for at in range(8, 8 + WHOLE_Z, CHUNK):
@@ -539,21 +576,22 @@
 
     apply_matrix(row_res[inner], 0)
     edges_start(lines.at[0], line_prev.at[0], line_next.at[0], 0)
-    send_back(0)
     weigh_refs[1][...] = row_cond[...] * lines[0]
     edges_wait(row_cond, cond_prev, cond_next, BASIS)
     line_diag()
+    operate_here(0)
     sums = product(sums, 0, lines[0, inner], row_res[inner])
 
     at = BASIS
     for k in range(BASIS):
         edges_wait(lines.at[k], line_prev.at[k], line_next.at[k], k)
-        operate(k)
+        operate_beside(k)
         if k < BASIS - 1:
             apply_matrix(image[k], k + 1, shift)
             edges_start(lines.at[k + 1], line_prev.at[k + 1], line_next.at[k + 1], k + 1)
-            send_back(k + 1)
+            send_back(k)
             weigh_refs[1][...] = row_cond[...] * lines[k + 1]
+            operate_here(k + 1)
             sums = product(sums, k + 1, lines[k + 1, inner], row_res[inner])
             for m in range(k + 1):
                 sums = product(sums, at, lines[m, inner], image[k])
@@ -565,13 +603,15 @@
         else:
             sums = product(sums, at, lines[k, inner], image[k])
 
-    def sum_over(sums, buf, n, me, peers):
+    def sum_over(sums, buf, n, me, peers, meanwhile=None):
         part[...] = sums
         buf[me] = sums
         for to in peers:
             pltpu.make_async_remote_copy(
                 src_ref=part, dst_ref=buf.at[me], send_sem=s_sum.at[n], recv_sem=r_sum.at[n],
                 device_id=to, device_id_type=MESH).start()
+        if meanwhile is not None:
+            meanwhile()
         got = buf.at[pl.ds(0, 15)]
         pltpu.make_async_copy(got, got, r_sum.at[n]).wait()
         pltpu.make_async_copy(got, got, s_sum.at[n]).wait()
@@ -585,7 +625,7 @@
                    key=lambda p: (-hops(p[0], 4) - hops(p[1], 4), p))
     sums = sum_over(sums, gather_a, 0, chip_x * 4 + chip_y, [
         ((gx // 8) * 8 + lax.rem(chip_x + x, 4) * 2 + core, lax.rem(chip_y + y, 4) * 2 + gy % 2)
-        for x, y in steps])
+        for x, y in steps], lambda: send_back(BASIS - 1))
     steps = sorted(((z, c) for z in range(8) for c in range(2) if (z, c) != (0, 0)),
                    key=lambda p: (-hops(p[0], 8) - 0.5 * p[1], p))
     peers = []
@@ -664,7 +704,7 @@
             pltpu.VMEM((EXT_Z, PAD_Y, COLS), f32),
             pltpu.VMEM((2, EXT_Z, PAD_Y, COLS), f32),
             pltpu.VMEM((PLANES, ROWS, COLS), f32),
-            pltpu.VMEM((WHOLE_Z, WHOLE_Z), f32),
+            pltpu.VMEM((2, WHOLE_Z, WHOLE_Z), jnp.bfloat16),
             pltpu.VMEM((ROWS, PLANES, COLS), f32),
             pltpu.VMEM((ROWS, PLANES, COLS), f32),
             pltpu.VMEM(line, f32),
@@ -686,7 +726,7 @@
             dma((BASIS,)), dma((BASIS,)), dma((2,)), dma((2,)), dma((5,)), pltpu.SemaphoreType.REGULAR,
         ],
         compiler_params=pltpu.CompilerParams(
-            collective_id=0, has_side_effects=True, vmem_limit_bytes=48 * 2**20),
+            collective_id=0, has_side_effects=True, vmem_limit_bytes=67043328),
     )(couplings, voltage, potential, tissue, gain, line_factor)
 
 

time: 98.7 us -> 90.5 us (0.917)
  local copies, waits for them, and re-layouts: 6.55 us -> 2.26 us
  Pallas kernels: 91.3 us -> 87.5 us
    unnamed x14 -> x4, local copies, waits for them, and re-layouts: 6.55 us -> 2.26 us
    pallas_call x1, Pallas kernels: 91.3 us -> 87.5 us  [body(): pl.pallas_call(kernel, name='bidomain', out_shape=(block, block), in_spec...]
where the time goes in v4:
time: 90.5 us; the launch traced here: 90.4 us
  Pallas kernels  87.5 us (97%)
  local copies, waits for them, and re-layouts  2.26 us (2%)
    pallas_call x1, Pallas kernels, body(): pl.pallas_call(kernel, name='bidomain', out_shape=(block, block), in_spec...  87.5 us
    unnamed x4, local copies, waits for them, and re-layouts  2.26 us

profile of v4, /device:TPU:1, one launch (start us, length us, event | category | flops | bytes accessed | tf_op | source)
XLA Modules:
  0.0 90.4 jit_solution(503080670551925340)
XLA Ops:
  0.6 87.5 %bidomain.1 = (f32[8,32,128]{2,1,0:T(8,128)}, f32[8,32,128]{2,1,0:T(8,128)}) custom-call(f32[2,9]{1,0:T(2,128)} %coup.1, f32[8,32,128]{2,1,0:T(8,128)} %volt_in.1, f32[8,32,128]{2,1,0:T(8,128)} %pot_in.1, s32[8,32,128]{2,1,0:T(8,128)} %tissue_in.1, f32[8,32,128]{2,1,0:T(8,128)} %gain_in.1, f32[256,256]{1,0:T(8,128)} %factor_in.1), custom_call_target="tpu_custom_call" | custom-call | tf_op jit(solution)/shard_map/bidomain/pallas_call | solution.py:688
  88.1 0.0 copy-start
  88.1 1.6 %copy.10 = f32[8,32,128]{2,1,0:T(8,128)} copy(f32[8,32,128]{2,1,0:T(8,128)} %get-tuple-element.4) | data formatting | bytes 262144
  89.7 0.0 copy-done
  89.7 0.7 copy.11
Async XLA Ops:
  88.1 1.6 %copy-start = (f32[8,32,128]{2,1,0:T(8,128)S(1)}, f32[8,32,128]{2,1,0:T(8,128)}, u32[]{:S(2)}) copy-start(f32[8,32,128]{2,1,0:T(8,128)} %get-tuple-element.5) | copy-start | bytes 393220

commit v5 on v4

--- a/solution.py
+++ b/solution.py
@@ -73,6 +73,12 @@
     out = k["lead"] * total
     out = out + k["both"] * (read(1, 1) + read(-1, -1)) + k["cross"] * (read(1, -1) + read(-1, 1))
     return out + shift_lanes(k["lead_sum"] * total, k["lead_diff"] * (plus - minus), first, last)
+
+
+def stencil_before(read, k, first, last):
+    minus = read(-1, 0)
+    out = k["lead"] * minus + k["both"] * read(-1, -1) + k["cross"] * read(-1, 1)
+    return out + shift_lanes(k["lead_sum"] * minus, -(k["lead_diff"] * minus), first, last)
 
 
 def stencil(read, k, first, last):
@@ -224,18 +230,23 @@
     upper = gy % 2 + turned * (1 - 2 * (gy % 2))
 
     def scatter_rows(stage, rows_ref, n):
-        for z in range(4):
-            for q in range(8):
-                m = z * 8 + (q if z % 2 == 0 else 7 - q)
-                t = m + turned * (31 - 2 * m)
-                to_gx, to_gy = upper * 16 + (z // 2) * 8 + q, chip_y * 2 + z % 2
-
-                @pl.when((to_gx != gx) | (to_gy != gy))
-                def _():
-                    pltpu.make_async_remote_copy(
-                        src_ref=stage.at[t], dst_ref=rows_ref.at[row_tile(gx)],
-                        send_sem=s_rows.at[n], recv_sem=r_rows.at[n],
-                        device_id=(to_gx, to_gy), device_id_type=MESH).start()
+        def one(d, _):
+            m = lax.rem(gx + d, 32)
+            z, q = m // 8, lax.rem(m, 8)
+            z_odd = lax.rem(z, 2)
+            to_gx = upper * 16 + (z // 2) * 8 + q + z_odd * (7 - 2 * q)
+            to_gy = chip_y * 2 + z_odd
+            t = m + turned * (31 - 2 * m)
+
+            @pl.when((to_gx != gx) | (to_gy != gy))
+            def _():
+                pltpu.make_async_remote_copy(
+                    src_ref=stage.at[t], dst_ref=rows_ref.at[row_tile(gx)],
+                    send_sem=s_rows.at[n], recv_sem=r_rows.at[n],
+                    device_id=(to_gx, to_gy), device_id_type=MESH).start()
+            return 0
+
+        lax.fori_loop(0, ROWS, one, 0, unroll=4)
 
         @pl.when(own_group)
         def _():
@@ -263,7 +274,9 @@
             pltpu.make_async_copy(stage, stage, s_rows.at[n]).wait()
 
     def send_back(k):
-        def one(i, _):
+        def one(d, _):
+            i = lax.rem(gx + d, GX)
+
             @pl.when((i != gx) | (own_gy != gy))
             def _():
                 pltpu.make_async_remote_copy(
@@ -292,41 +305,47 @@
 
     inner = LINES
 
-    def edge(src, dst, n, side):
+    HALF = WHOLE_Z // 2
+
+    def edge(src, dst, n, side, part):
         to_gx, to_gy = owner(row + (1 if side == 0 else -1))
+        rows = pl.ds(8 + part * HALF, HALF)
         return pltpu.make_async_remote_copy(
-            src_ref=src.at[inner], dst_ref=dst.at[inner],
-            send_sem=s_edge.at[n, side], recv_sem=r_edge.at[n, side],
+            src_ref=src.at[rows], dst_ref=dst.at[rows],
+            send_sem=s_edge.at[n, side, part], recv_sem=r_edge.at[n, side, part],
             device_id=(to_gx, to_gy), device_id_type=MESH)
 
     has_next, has_prev = row < WHOLE_Y - 1, row > 0
 
-    def edges_start(src, prev, nxt, n):
+    def edges_start(src, prev, nxt, n, part):
         @pl.when(has_next)
         def _():
-            edge(src, prev, n, 0).start()
-
+            edge(src, prev, n, 0, part).start()
+
+        if n != BASIS - 1:
+            @pl.when(has_prev)
+            def _():
+                edge(src, nxt, n, 1, part).start()
+
+    def edges_wait(src, prev, nxt, n, part):
         @pl.when(has_prev)
         def _():
-            edge(src, nxt, n, 1).start()
-
-    def edges_wait(src, prev, nxt, n):
-        @pl.when(has_prev)
-        def _():
-            edge(src, prev, n, 0).wait_recv()
-
+            edge(src, prev, n, 0, part).wait_recv()
+
+        if n != BASIS - 1:
+            @pl.when(has_next)
+            def _():
+                edge(src, nxt, n, 1, part).wait_recv()
+
+    def edges_sent(src, prev, nxt, n, part):
         @pl.when(has_next)
         def _():
-            edge(src, nxt, n, 1).wait_recv()
-
-    def edges_sent(src, prev, nxt, n):
-        @pl.when(has_next)
-        def _():
-            edge(src, prev, n, 0).wait_send()
-
-        @pl.when(has_prev)
-        def _():
-            edge(src, nxt, n, 1).wait_send()
+            edge(src, prev, n, 0, part).wait_send()
+
+        if n != BASIS - 1:
+            @pl.when(has_prev)
+            def _():
+                edge(src, nxt, n, 1, part).wait_send()
 
     own_y = pl.ds(OWN, ROWS)
     conduct = tissue[...].astype(jnp.float32) * gain[...]
@@ -471,37 +490,41 @@
 
     lax.fori_loop(0, EXT_Z, first_update, 0)
 
-    def sweep(n, weight):
+    def sweep(n, weight, margin):
         old = weighted.at[lax.rem(n + 1, 2)]
         new = lax.rem(n, 2)
         weight_next = 1.0 / (2.0 * ratio - weight)
         keep = weight_next * weight
         gain_r = 2.0 * weight_next / half
+        at, count = OWN - margin, ROWS + 2 * margin
+        rows = pl.ds(at, count)
 
         def one(z):
-            u = upd[z, EXT, :]
-            c = cond[z, EXT, :]
-            r = resid[z, EXT, :] - diag[z, EXT, :] * u + c * stencil(moved(old, z, 8, EXT_Y), z_twice, first, last)
+            u = upd[z, rows, :]
+            c = cond[z, rows, :]
+            r = resid[z, rows, :] - diag[z, rows, :] * u + c * stencil(moved(old, z, at, count), z_twice, first, last)
             fresh = keep * u + gain_r * r
-            return r, fresh, estimate[z, EXT, :] + fresh, c * fresh
+            return r, fresh, estimate[z, rows, :] + fresh, c * fresh
 
         def pair(i, _):
             planes = [n + 2 * i, n + 2 * i + 1]
             for z, (r, fresh, total, flux) in zip(planes, [one(z) for z in planes]):
-                resid[z, EXT, :] = r
-                upd[z, EXT, :] = fresh
-                estimate[z, EXT, :] = total
-                weighted[new, z, EXT, :] = flux
+                resid[z, rows, :] = r
+                upd[z, rows, :] = fresh
+                estimate[z, rows, :] = total
+                weighted[new, z, rows, :] = flux
             return 0
 
         lax.fori_loop(0, EXT_Z // 2 - n, pair, 0)
         return weight_next
 
     each_halo(wait_send, resid, HALO, s_resid, r_resid, False)
-    weight = lax.fori_loop(1, CHEB - 2, sweep, weight)
+    weight = lax.fori_loop(1, 4, lambda n, w: sweep(n, w, 8), weight)
+    weight = lax.fori_loop(4, CHEB - 2, lambda n, w: sweep(n, w, 4), weight)
     wait_rows(stage_cond, row_cond, 0)
-    edges_start(row_cond, cond_prev, cond_next, BASIS)
-    lax.fori_loop(CHEB - 2, CHEB, sweep, weight)
+    for half_line in range(2):
+        edges_start(row_cond, cond_prev, cond_next, BASIS, half_line)
+    lax.fori_loop(CHEB - 2, CHEB, lambda n, w: sweep(n, w, 4), weight)
 
     def total_plane(z, _):
         total = fields[0, z, EXT, :] + estimate[z, EXT, :]
@@ -521,7 +544,9 @@
     stage_res[...] = jnp.swapaxes(own_term[...], 0, 1)
     scatter_rows(stage_res, row_res, 1)
 
-    new_volt[...] = volt[...] + estimate[pl.ds(HALO, PLANES), own_y, :]
+    gain[...] = volt[...] + estimate[pl.ds(HALO, PLANES), own_y, :]
+    early = pltpu.make_async_copy(gain, new_volt, s_take.at[0])
+    early.start()
     wait_rows(stage_res, row_res, 1)
 
     def apply_matrix(src, k, shift=None):
@@ -531,10 +556,13 @@
         def dot(a, b):
             return jnp.dot(a, b, preferred_element_type=jnp.float32)
 
-        out = dot(matrix[0], fine) + dot(matrix[1], coarse) + dot(matrix[0], coarse)
-        if shift is not None:
-            out = out - shift * lines[k - 1, LINES]
-        lines[k, LINES] = out
+        for part in range(2):
+            rows = pl.ds(part * HALF, HALF)
+            out = dot(matrix[0, rows], fine) + dot(matrix[1, rows], coarse) + dot(matrix[0, rows], coarse)
+            if shift is not None:
+                out = out - shift * lines[k - 1, pl.ds(8 + part * HALF, HALF)]
+            lines[k, pl.ds(8 + part * HALF, HALF)] = out
+            edges_start(lines.at[k], line_prev.at[k], line_next.at[k], k, part)
 
     sums = jnp.zeros((1, COLS), jnp.float32)
 
@@ -561,13 +589,19 @@
 
     def operate_beside(k):
         basis = [line_prev.at[k], None, line_next.at[k]]
-        for n in (0, 2):
-            weigh_refs[n][...] = cond_refs[n][...] * basis[n][...]
-        for at in range(8, 8 + WHOLE_Z, CHUNK):
-            rows = pl.ds(at, CHUNK)
-            ki = row_cond[rows] * stencil_beside(near_rows(weigh_refs, at), line_in, first, last)
-            ki = ki + stencil_beside(near_rows(basis, at), line_ex, first, last)
-            image[k, pl.ds(at - 8, CHUNK)] = image[k, pl.ds(at - 8, CHUNK)] - ki
+        split = 8 + HALF
+        for part, lined in enumerate((pl.ds(0, split), pl.ds(split, LINE - split))):
+            edges_wait(lines.at[k], line_prev.at[k], line_next.at[k], k, part)
+            for n in (0, 2) if k < BASIS - 1 else (0,):
+                weigh_refs[n][lined] = cond_refs[n][lined] * basis[n][lined]
+            for at in (range(8, split - CHUNK, CHUNK) if part == 0 else range(split - CHUNK, 8 + WHOLE_Z, CHUNK)):
+                rows = pl.ds(at, CHUNK)
+                beside = stencil_beside if k < BASIS - 1 else stencil_before
+                ki = row_cond[rows] * beside(near_rows(weigh_refs, at), line_in, first, last)
+                ki = ki + beside(near_rows(basis, at), line_ex, first, last)
+                if k == BASIS - 1:
+                    ki = 2.0 * ki
+                image[k, pl.ds(at - 8, CHUNK)] = image[k, pl.ds(at - 8, CHUNK)] - ki
 
     def line_diag():
         for at in range(8, 8 + WHOLE_Z, CHUNK):
@@ -575,21 +609,20 @@
             row_diag[rows] = ex_total + row_cond[rows] * stencil(near_rows(cond_refs, at), line_in, first, last)
 
     apply_matrix(row_res[inner], 0)
-    edges_start(lines.at[0], line_prev.at[0], line_next.at[0], 0)
+    send_back(0)
     weigh_refs[1][...] = row_cond[...] * lines[0]
-    edges_wait(row_cond, cond_prev, cond_next, BASIS)
+    for half_line in range(2):
+        edges_wait(row_cond, cond_prev, cond_next, BASIS, half_line)
     line_diag()
     operate_here(0)
     sums = product(sums, 0, lines[0, inner], row_res[inner])
 
     at = BASIS
     for k in range(BASIS):
-        edges_wait(lines.at[k], line_prev.at[k], line_next.at[k], k)
         operate_beside(k)
         if k < BASIS - 1:
             apply_matrix(image[k], k + 1, shift)
-            edges_start(lines.at[k + 1], line_prev.at[k + 1], line_next.at[k + 1], k + 1)
-            send_back(k)
+            send_back(k + 1)
             weigh_refs[1][...] = row_cond[...] * lines[k + 1]
             operate_here(k + 1)
             sums = product(sums, k + 1, lines[k + 1, inner], row_res[inner])
@@ -603,15 +636,13 @@
         else:
             sums = product(sums, at, lines[k, inner], image[k])
 
-    def sum_over(sums, buf, n, me, peers, meanwhile=None):
+    def sum_over(sums, buf, n, me, peers):
         part[...] = sums
         buf[me] = sums
         for to in peers:
             pltpu.make_async_remote_copy(
                 src_ref=part, dst_ref=buf.at[me], send_sem=s_sum.at[n], recv_sem=r_sum.at[n],
                 device_id=to, device_id_type=MESH).start()
-        if meanwhile is not None:
-            meanwhile()
         got = buf.at[pl.ds(0, 15)]
         pltpu.make_async_copy(got, got, r_sum.at[n]).wait()
         pltpu.make_async_copy(got, got, s_sum.at[n]).wait()
@@ -625,7 +656,7 @@
                    key=lambda p: (-hops(p[0], 4) - hops(p[1], 4), p))
     sums = sum_over(sums, gather_a, 0, chip_x * 4 + chip_y, [
         ((gx // 8) * 8 + lax.rem(chip_x + x, 4) * 2 + core, lax.rem(chip_y + y, 4) * 2 + gy % 2)
-        for x, y in steps], lambda: send_back(BASIS - 1))
+        for x, y in steps])
     steps = sorted(((z, c) for z in range(8) for c in range(2) if (z, c) != (0, 0)),
                    key=lambda p: (-hops(p[0], 8) - 0.5 * p[1], p))
     peers = []
@@ -670,13 +701,15 @@
         total = total + sol[k] * back[k]
     new_pot[...] = pot[...] + jnp.swapaxes(total, 0, 1)
 
+    early.wait()
     each_deep(wait_send)
     each_halo(wait_send, fields.at[2], 1, s_pot, r_pot, False)
     wait_rows_sent(stage_cond, 0)
     wait_rows_sent(stage_res, 1)
-    edges_sent(row_cond, cond_prev, cond_next, BASIS)
-    for k in range(BASIS):
-        edges_sent(lines.at[k], line_prev.at[k], line_next.at[k], k)
+    for half_line in range(2):
+        edges_sent(row_cond, cond_prev, cond_next, BASIS, half_line)
+        for k in range(BASIS):
+            edges_sent(lines.at[k], line_prev.at[k], line_next.at[k], k, half_line)
 
 
 def body(voltage, potential, tissue, gain, couplings, line_factor):
@@ -690,7 +723,7 @@
         name="bidomain",
         out_shape=(block, block),
         in_specs=[pl.BlockSpec(memory_space=pltpu.SMEM)] + [pl.BlockSpec(memory_space=pl.ANY)] * 5,
-        out_specs=(vmem, vmem),
+        out_specs=(pl.BlockSpec(memory_space=pl.ANY), vmem),
         scratch_shapes=[
             pltpu.VMEM((PLANES, ROWS, COLS), f32),
             pltpu.VMEM((PLANES, ROWS, COLS), f32),
@@ -722,7 +755,7 @@
             pltpu.VMEM((16, 1, COLS), f32),
             pltpu.VMEM((16, 1, COLS), f32),
             dma((8,)), dma((8,)), dma((8,)), dma((8,)), dma((8,)), dma((8,)), dma((8,)), dma((8,)),
-            dma((2,)), dma((2,)), dma((BASIS + 1, 2)), dma((BASIS + 1, 2)),
+            dma((2,)), dma((2,)), dma((BASIS + 1, 2, 2)), dma((BASIS + 1, 2, 2)),
             dma((BASIS,)), dma((BASIS,)), dma((2,)), dma((2,)), dma((5,)), pltpu.SemaphoreType.REGULAR,
         ],
         compiler_params=pltpu.CompilerParams(

time: 90.5 us -> 88.9 us (0.982)
  Pallas kernels: 87.5 us -> 85.8 us
    pallas_call x1, Pallas kernels: 87.5 us -> 85.8 us  [body(): pl.pallas_call(kernel, name='bidomain', out_shape=(block, block), in_spec...]
where the time goes in v5:
time: 88.9 us; the launch traced here: 88.7 us
  Pallas kernels  85.8 us (97%)
  local copies, waits for them, and re-layouts  2.26 us (3%)
    pallas_call x1, Pallas kernels, body(): pl.pallas_call(kernel, name='bidomain', out_shape=(block, block), in_spec...  85.8 us
    unnamed x4, local copies, waits for them, and re-layouts  2.26 us

profile of v5, /device:TPU:1, one launch (start us, length us, event | category | flops | bytes accessed | tf_op | source)
XLA Modules:
  0.0 88.7 jit_solution(16594576213437741152)
XLA Ops:
  0.6 85.8 %bidomain.1 = (f32[8,32,128]{2,1,0:T(8,128)}, f32[8,32,128]{2,1,0:T(8,128)}) custom-call(f32[2,9]{1,0:T(2,128)} %coup.1, f32[8,32,128]{2,1,0:T(8,128)} %volt_in.1, f32[8,32,128]{2,1,0:T(8,128)} %pot_in.1, s32[8,32,128]{2,1,0:T(8,128)} %tissue_in.1, f32[8,32,128]{2,1,0:T(8,128)} %gain_in.1, f32[256,256]{1,0:T(8,128)} %factor_in.1), custom_call_target="tpu_custom_call" | custom-call | tf_op jit(solution)/shard_map/bidomain/pallas_call | solution.py:721
  86.5 0.0 copy-start
  86.5 1.6 %copy.10 = f32[8,32,128]{2,1,0:T(8,128)} copy(f32[8,32,128]{2,1,0:T(8,128)} %get-tuple-element.4) | data formatting | bytes 262144
  88.1 0.0 copy-done
  88.1 0.7 copy.11
Async XLA Ops:
  86.5 1.6 %copy-start = (f32[8,32,128]{2,1,0:T(8,128)S(1)}, f32[8,32,128]{2,1,0:T(8,128)}, u32[]{:S(2)}) copy-start(f32[8,32,128]{2,1,0:T(8,128)} %get-tuple-element.5) | copy-start | bytes 393220

commit v6 on v5

--- a/solution.py
+++ b/solution.py
@@ -467,6 +467,8 @@
         return 0
 
     lax.fori_loop(HALO, HALO + PLANES, extra_plane, 0)
+    pl.semaphore_wait(far, 10)
+    scatter_rows(stage_cond, row_cond, 0)
     each_deep(wait_recv, receive=True)
 
     def diag_plane(z, _):
@@ -475,8 +477,6 @@
 
     lax.fori_loop(1, EXT_Z - 1, diag_plane, 0)
     each_halo(wait_send, near, 1, s_fields, r_fields, True)
-    pl.semaphore_wait(far, 10)
-    scatter_rows(stage_cond, row_cond, 0)
     each_halo(wait_recv, resid, HALO, s_resid, r_resid, False, receive=True)
 
     inv_centre = 1.0 / centre

time: 88.9 us -> 88.7 us (level)
  no operation moved by 1% of the time
where the time goes in v6:
time: 88.7 us; the launch traced here: 88.6 us
  Pallas kernels  85.7 us (97%)
  local copies, waits for them, and re-layouts  2.26 us (3%)
    pallas_call x1, Pallas kernels, body(): pl.pallas_call(kernel, name='bidomain', out_shape=(block, block), in_spec...  85.7 us
    unnamed x4, local copies, waits for them, and re-layouts  2.26 us

profile of v6, /device:TPU:1, one launch (start us, length us, event | category | flops | bytes accessed | tf_op | source)
XLA Modules:
  0.0 88.6 jit_solution(4788305533771703593)
XLA Ops:
  0.6 85.7 %bidomain.1 = (f32[8,32,128]{2,1,0:T(8,128)}, f32[8,32,128]{2,1,0:T(8,128)}) custom-call(f32[2,9]{1,0:T(2,128)} %coup.1, f32[8,32,128]{2,1,0:T(8,128)} %volt_in.1, f32[8,32,128]{2,1,0:T(8,128)} %pot_in.1, s32[8,32,128]{2,1,0:T(8,128)} %tissue_in.1, f32[8,32,128]{2,1,0:T(8,128)} %gain_in.1, f32[256,256]{1,0:T(8,128)} %factor_in.1), custom_call_target="tpu_custom_call" | custom-call | tf_op jit(solution)/shard_map/bidomain/pallas_call | solution.py:721
  86.3 0.0 copy-start
  86.3 1.6 %copy.10 = f32[8,32,128]{2,1,0:T(8,128)} copy(f32[8,32,128]{2,1,0:T(8,128)} %get-tuple-element.4) | data formatting | bytes 262144
  87.9 0.0 copy-done
  87.9 0.7 copy.11
Async XLA Ops:
  86.3 1.6 %copy-start = (f32[8,32,128]{2,1,0:T(8,128)S(1)}, f32[8,32,128]{2,1,0:T(8,128)}, u32[]{:S(2)}) copy-start(f32[8,32,128]{2,1,0:T(8,128)} %get-tuple-element.5) | copy-start | bytes 393220

commit v7 on v6

--- a/solution.py
+++ b/solution.py
@@ -356,8 +356,8 @@
     pl.semaphore_wait(barrier, 25)
     near = fields.at[pl.ds(0, 2)]
     each_halo(start, near, 1, s_fields, r_fields, True)
+    each_deep(start)
     each_halo(start, fields.at[2], 1, s_pot, r_pot, False)
-    each_deep(start)
     for d in range(1, 8):
         greet(far, at_z(lax.rem(chip_z + d, 8)))
     for d in range(1, 4):
@@ -458,6 +458,15 @@
     lax.fori_loop(HALO, HALO + PLANES, first_plane, 0)
     each_halo(start, resid, HALO, s_resid, r_resid, False)
 
+    pl.semaphore_wait(far, 10)
+    scatter_rows(stage_cond, row_cond, 0)
+    each_deep(wait_recv, receive=True)
+
+    def diag_plane(z, _):
+        diag[z, EXT, :] = 1.0 + cond[z, EXT, :] * stencil(moved(cond, z, 8, EXT_Y), z_twice, first, last)
+        return 0
+
+    lax.fori_loop(1, EXT_Z - 1, diag_plane, 0)
     each_halo(wait_recv, fields.at[2], 1, s_pot, r_pot, False, receive=True)
     ex_total = 2.0 * ex_sum
 
@@ -467,15 +476,6 @@
         return 0
 
     lax.fori_loop(HALO, HALO + PLANES, extra_plane, 0)
-    pl.semaphore_wait(far, 10)
-    scatter_rows(stage_cond, row_cond, 0)
-    each_deep(wait_recv, receive=True)
-
-    def diag_plane(z, _):
-        diag[z, EXT, :] = 1.0 + cond[z, EXT, :] * stencil(moved(cond, z, 8, EXT_Y), z_twice, first, last)
-        return 0
-
-    lax.fori_loop(1, EXT_Z - 1, diag_plane, 0)
     each_halo(wait_send, near, 1, s_fields, r_fields, True)
     each_halo(wait_recv, resid, HALO, s_resid, r_resid, False, receive=True)
 

time: 88.7 us -> 88.7 us (level)
  no operation moved by 1% of the time
where the time goes in v7:
time: 88.7 us; the launch traced here: 88.6 us
  Pallas kernels  85.7 us (97%)
  local copies, waits for them, and re-layouts  2.26 us (3%)
    pallas_call x1, Pallas kernels, body(): pl.pallas_call(kernel, name='bidomain', out_shape=(block, block), in_spec...  85.7 us
    unnamed x4, local copies, waits for them, and re-layouts  2.26 us

profile of v7, /device:TPU:1, one launch (start us, length us, event | category | flops | bytes accessed | tf_op | source)
XLA Modules:
  0.0 88.6 jit_solution(10078917687711953533)
XLA Ops:
  0.6 85.7 %bidomain.1 = (f32[8,32,128]{2,1,0:T(8,128)}, f32[8,32,128]{2,1,0:T(8,128)}) custom-call(f32[2,9]{1,0:T(2,128)} %coup.1, f32[8,32,128]{2,1,0:T(8,128)} %volt_in.1, f32[8,32,128]{2,1,0:T(8,128)} %pot_in.1, s32[8,32,128]{2,1,0:T(8,128)} %tissue_in.1, f32[8,32,128]{2,1,0:T(8,128)} %gain_in.1, f32[256,256]{1,0:T(8,128)} %factor_in.1), custom_call_target="tpu_custom_call" | custom-call | tf_op jit(solution)/shard_map/bidomain/pallas_call | solution.py:721
  86.3 0.0 copy-start
  86.3 1.6 %copy.10 = f32[8,32,128]{2,1,0:T(8,128)} copy(f32[8,32,128]{2,1,0:T(8,128)} %get-tuple-element.4) | data formatting | bytes 262144
  87.9 0.0 copy-done
  87.9 0.7 copy.11
Async XLA Ops:
  86.3 1.6 %copy-start = (f32[8,32,128]{2,1,0:T(8,128)S(1)}, f32[8,32,128]{2,1,0:T(8,128)}, u32[]{:S(2)}) copy-start(f32[8,32,128]{2,1,0:T(8,128)} %get-tuple-element.5) | copy-start | bytes 393220
